TPU v7x, 512 devices: a whole 4x8x8 slice. The times are simulated.
512 devices in a mesh: batch: 32 (over y_lo, z), seq: 16 (over y_hi, x, core).
Axes of the slice: x: 4, y: 8 (y_hi: 2, y_lo: 4; y = y_hi * 4 + y_lo), z: 8, core: 2. Of those that a mesh axis runs over, the one named last changes fastest.
Arguments:
- sequence_input: bfloat16 [32, 4096, 768], P('batch', 'seq'), may hold values from -64 to 64
- bn_gain: float32 [768], replicated, may hold values from 0.1 to 1.9
- bn_bias: float32 [768], replicated, may hold values from -3 to 3
- conv_weight: bfloat16 [5, 768, 768], P(None, None, 'batch'), may hold values from -0.09375 to 0.09375
- conv_bias: float32 [768], replicated, may hold values from -3 to 3
- ln_gain: float32 [768], replicated, may hold values from 0.1 to 1.9
- ln_bias: float32 [768], replicated, may hold values from -3 to 3
- qkv_weight: bfloat16 [768, 1792], P(None, 'batch'), may hold values from -32 to 32
Outputs:
- pooled: bfloat16 [32, 2048, 768], P('batch', 'seq')
- attended: bfloat16 [32, 2048, 768], P('batch', 'seq')
All inputs are finite; a program needn't handle non-finite values.
Results may differ from a plain program's by a relative error of at most 0.025.
The roundings to bfloat16 on the way count: a program that leaves them out, or rounds other values in their place, can miss the bound.
Values may be sent and summed in bfloat16 or wider, within the bound.
No kernel may reach another device: no remote copies, remote signals or barrier semaphores. Data moves between devices by JAX's collectives and lax.ppermute only.
A program may use at most 64 MiB of HBM per device.

v0:
```python
import jax
import jax.numpy as jnp
from jax import lax
from jax.sharding import PartitionSpec as P

HEADS = 8
KEY = 64
VAL = 96


epsilon = 1e-05


def extended(cells, sides, width):
    for axis, dim in sides:
        count = lax.axis_size(axis)
        ends = count - 1
        head = lax.slice_in_dim(cells, 0, width, axis=dim)
        tail = lax.slice_in_dim(cells, cells.shape[dim] - width, cells.shape[dim], axis=dim)
        cells = jnp.concatenate(
            [
                lax.ppermute(tail, axis, [(i, (i + 1) % count) for i in range(ends)]),
                cells,
                lax.ppermute(head, axis, [((i + 1) % count, i) for i in range(ends)]),
            ],
            axis=dim,
        )
    return cells


def conv_taps(padded, kernel, positions):
    result = None
    for tap_index in range(kernel.shape[0]):
        window = padded[:, tap_index : tap_index + positions]
        product = jnp.einsum(
            "slc,co->slo", window, kernel[tap_index], preferred_element_type=jnp.float32
        )
        result = product if result is None else result + product
    return result


def online_step(carry, query_rows, key_block, value_block):
    best, weight_sum, accum = carry
    scores = jnp.einsum(
        "sqhk,sjhk->shqj", query_rows, key_block, preferred_element_type=jnp.float32
    )
    newest = jnp.maximum(best, jnp.max(scores, axis=-1))
    fade = jnp.exp(best - newest)
    weights = jnp.exp(scores - newest[..., None])
    weight_sum = weight_sum * fade + jnp.sum(weights, axis=-1)
    accum = accum * fade[..., None] + jnp.einsum(
        "shqj,sjhv->shqv",
        weights.astype(jnp.bfloat16),
        value_block,
        preferred_element_type=jnp.float32,
    )
    return (newest, weight_sum, accum)


def blocked_attend(carry, query_rows, key_piece, value_piece):
    rows = key_piece.shape[1]
    block = min(rows, 512)
    for first in range(0, rows, block):
        carry = online_step(
            carry,
            query_rows,
            key_piece[:, first : first + block],
            value_piece[:, first : first + block],
        )
    return carry


def empty_state(seqs_here, heads_here, rows):
    return (
        jnp.full((seqs_here, heads_here, rows), -jnp.inf, jnp.float32),
        jnp.zeros((seqs_here, heads_here, rows), jnp.float32),
        jnp.zeros((seqs_here, heads_here, rows, VAL), jnp.float32),
    )


def on_device(
    sequence_input, bn_gain, bn_bias, conv_weight, conv_bias, ln_gain, ln_bias, qkv_weight
):
    seqs_here = sequence_input.shape[0]
    positions = sequence_input.shape[1]
    channels = sequence_input.shape[2]
    values_in = sequence_input.astype(jnp.float32)
    total, squares = lax.psum(
        (jnp.sum(values_in, axis=(0, 1)), jnp.sum(values_in * values_in, axis=(0, 1))),
        ("batch", "seq"),
    )
    count = float(seqs_here * positions * lax.axis_size("batch") * lax.axis_size("seq"))
    mean = total / count
    var = squares / count - mean * mean
    activated = jax.nn.gelu(
        (values_in - mean) * lax.rsqrt(var + epsilon) * bn_gain + bn_bias, approximate=True
    ).astype(jnp.bfloat16)
    padded = extended(activated, (("seq", 1),), 2)
    conv_out = conv_taps(
        padded, lax.all_gather(conv_weight, "batch", axis=2, tiled=True), positions
    )
    conv_out = conv_out + conv_bias
    bins_here = positions // 2
    pooled = conv_out.reshape(seqs_here, bins_here, 2, channels).max(axis=2).astype(jnp.bfloat16)
    pooled_wide = pooled.astype(jnp.float32)
    centre = jnp.mean(pooled_wide, axis=-1, keepdims=True)
    spread = jnp.mean((pooled_wide - centre) ** 2, axis=-1, keepdims=True)
    normed = ((pooled_wide - centre) * lax.rsqrt(spread + epsilon) * ln_gain + ln_bias).astype(
        jnp.bfloat16
    )
    proj = jnp.einsum(
        "sbd,dk->sbk",
        normed,
        lax.all_gather(qkv_weight, "batch", axis=1, tiled=True),
        preferred_element_type=jnp.float32,
    )
    head_keys = HEADS * KEY
    queries = (proj[..., :head_keys] * KEY ** (-0.5)).astype(jnp.bfloat16)
    key_rows = proj[..., head_keys : 2 * head_keys].astype(jnp.bfloat16)
    value_rows = proj[..., 2 * head_keys :].astype(jnp.bfloat16)
    query_heads = queries.reshape(seqs_here, bins_here, HEADS, KEY)
    key_piece = lax.all_gather(key_rows, "seq", axis=1, tiled=True)
    value_piece = lax.all_gather(value_rows, "seq", axis=1, tiled=True)
    width_now = key_piece.shape[1]
    best, weight_sum, accum = blocked_attend(
        empty_state(seqs_here, HEADS, bins_here),
        query_heads,
        key_piece.reshape(seqs_here, width_now, HEADS, KEY),
        value_piece.reshape(seqs_here, width_now, HEADS, VAL),
    )
    attended = (
        (accum / weight_sum[..., None])
        .transpose(0, 2, 1, 3)
        .reshape(seqs_here, bins_here, HEADS * VAL)
        .astype(jnp.bfloat16)
    )
    return (pooled, attended)


def solution(mesh):
    placed = (
        P("batch", "seq", None),
        P(),
        P(),
        P(None, None, "batch"),
        P(),
        P(),
        P(),
        P(None, "batch"),
    )
    return jax.shard_map(
        on_device,
        mesh=mesh,
        in_specs=placed,
        out_specs=(P("batch", "seq", None), P("batch", "seq", None)),
        check_vma=False,
    )
```

profile of v0, /device:TPU:8, one launch (start us, length us, event | category | flops | bytes accessed | tf_op | source)
XLA Modules:
  0.0 494.3 jit_solution(5999719984073595939)
XLA Ops:
  7.9 0.7 all-gather.7.cloned.1.call-update
  8.7 1.1 convert_reduce_fusion
  9.8 110.0 %all-reduce = (f32[768]{0:T(1024)S(1)}, f32[768]{0:T(1024)S(1)}) all-reduce(f32[768]{0:T(1024)S(1)} %get-tuple-element.7, f32[768]{0:T(1024)S(1)} %get-tuple-element.6), channel_id=1, replica_groups=mesh['batch'=32,'seq'=16] {'batch','seq'}, use_global_device_ids=true, to_apply=%region_3.0 | all-reduce | flops 1536 | bytes 12288 | tf_op jit(solution)/shard_map/psum | solution.py:88
  119.8 1.4 fusion.28
  121.2 1.7 collective-permute-start
  122.9 1.3 collective-permute-start.1
  124.2 47.6 %all-gather.5.cloned.1.call-done = bf16[5,768,768]{1,2,0:T(8,128)(2,1)} async-done(((bf16[5,768,24]{1,2,0:T(8,128)(2,1)}), bf16[5,768,768]{1,2,0:T(8,128)(2,1)}) %all-gather.5.cloned.1.call-update) | async-done | bytes 5898256 | tf_op jit(solution)/shard_map/all_gather | solution.py:100
  171.9 1.9 fusion.13
  173.8 1.9 convolution_add_fusion.3
  177.6 1.0 reduce_max.45
  179.0 147.5 %all-gather.7.cloned.1.call-done = bf16[768,1792]{0,1:T(8,128)(2,1)} async-done(((bf16[768,56]{0,1:T(8,128)(2,1)}), bf16[768,1792]{0,1:T(8,128)(2,1)}) %all-gather.7.cloned.1.call-update) | async-done | bytes 2752528 | tf_op jit(solution)/shard_map/all_gather | solution.py:114
  326.5 2.8 fusion.69
  331.1 69.4 %all-gather.9.cloned.1.call-done = bf16[1,2048,512]{2,1,0:T(8,128)(2,1)} async-done(((bf16[1,128,512]{2,1,0:T(8,128)(2,1)}), bf16[1,2048,512]{2,1,0:T(8,128)(2,1)}) %all-gather.9.cloned.1.call-update) | async-done | bytes 2097168 | tf_op jit(solution)/shard_map/all_gather | solution.py:122
  400.5 2.9 copy.24
  403.5 1.4 copy-done.6
  405.4 2.2 fusion.72
  409.1 1.2 fusion
  410.4 1.2 fusion.2
  411.6 64.0 %all-gather.11.cloned.1.call-done = bf16[1,2048,768]{2,1,0:T(8,128)(2,1)} async-done(((bf16[1,128,768]{2,1,0:T(8,128)(2,1)}), bf16[1,2048,768]{2,1,0:T(8,128)(2,1)}) %all-gather.11.cloned.1.call-update) | async-done | bytes 3145744 | tf_op jit(solution)/shard_map/all_gather | solution.py:123
  475.6 4.7 copy.25
  480.3 2.5 fusion.12
  482.8 1.8 fusion.11
  485.5 0.8 copy-done.5
  486.9 0.8 copy.26
  (54 shorter events, 8.4 us)
Async XLA Ops:
  7.2 164.7 %all-gather.5.cloned.1.call-start = ((), (), s32[]{:S(2)}) async-start(), calls=%async_computation | async-start | bytes 6082560 | tf_op jit(solution)/shard_map/all_gather | solution.py:100
  7.9 318.6 %all-gather.7.cloned.1.call-start = ((), (), s32[]{:S(2)}) async-start(), calls=%async_computation.1 | async-start | bytes 2838528 | tf_op jit(solution)/shard_map/all_gather | solution.py:114
  8.6 391.9 %all-gather.9.cloned.1.call-start = ((), (), s32[]{:S(2)}) async-start(), calls=%async_computation.2 | async-start | bytes 2228224 | tf_op jit(solution)/shard_map/all_gather | solution.py:122
  121.2 3.0 collective-permute-start
  122.9 53.3 %collective-permute-start.1 = (bf16[1,2,768]{2,1,0:T(2,128)(2,1)S(1)}, bf16[1,2,768]{2,1,0:T(2,128)(2,1)S(1)}, u32[]{:S(2)}, u32[]{:S(2)}) collective-permute-start(bf16[1,2,768]{2,1,0:T(2,128)(2,1)S(1)} %get-tuple-element.17), channel_id=1, source_target_pairs={{1,0},{2,1},{3,2},{4,3},{5,4},{6,5},{7,6},{8,7},{9,8},{10,9},{11,1... | collective-permute-start | bytes 9224 | tf_op jit(solution)/shard_map/ppermute | solution.py:24
  171.8 3.9 copy-start.9
  176.2 0.7 copy-start.12
  176.9 149.6 %copy-start.10 = (f32[768]{0:T(1024)S(1)}, f32[768]{0:T(1024)}, u32[]{:S(2)}) copy-start(f32[768]{0:T(1024)} %param.14) | copy-start | bytes 9220
  176.9 149.6 %copy-start.11 = (f32[768]{0:T(1024)S(1)}, f32[768]{0:T(1024)}, u32[]{:S(2)}) copy-start(f32[768]{0:T(1024)} %param.13) | copy-start | bytes 9220
  178.6 150.7 %copy-start.8 = (bf16[128,768]{1,0:T(8,128)(2,1)}, bf16[128,768]{1,0:T(8,128)(2,1)S(1)}, u32[]{:S(2)}) copy-start(bf16[128,768]{1,0:T(8,128)(2,1)S(1)} %reduce_max.45) | copy-start | bytes 589828
  330.0 145.6 %all-gather.11.cloned.1.call-start = ((), (), s32[]{:S(2)}) async-start(), calls=%async_computation.3 | async-start | bytes 3342336 | tf_op jit(solution)/shard_map/all_gather | solution.py:123
  403.5 1.4 copy-start.6
  405.4 3.7 copy-start.4
  405.4 2.5 copy-start.7
  408.5 2.0 copy-start
  409.0 1.4 copy-start.2
  480.3 2.5 copy-start.1
  482.8 2.1 copy-start.3
  484.6 1.7 copy-start.5
Sparse Core Ops, SparseCore 0:
  10.1 161.7 all-gather.4
  173.9 152.5 all-gather.6
  330.1 70.3 all-gather.8
  404.3 71.2 all-gather.10
where the time goes:
time: 495 us; the launch traced here: 494 us
  waiting for transfers between devices  330 us (67%)
  blocking collectives  110 us (22%)
  matrix products  17.6 us (4%)
  between operations  14 us (3%)
  local copies, waits for them, and re-layouts  13.2 us (3%)
  other arithmetic  6.26 us (1%)
    all_gather x1, waiting for transfers between devices, on_device(): lax.all_gather(qkv_weight, 'batch', axis=1, tiled=True)  147 us
    psum x1, blocking collectives, on_device(): lax.psum((jnp.sum(values_in, axis=(0, 1)), jnp.sum(values_in * values_in,...  110 us
    all_gather x1, waiting for transfers between devices, on_device(): key_piece = lax.all_gather(key_rows, 'seq', axis=1, tiled=True)  69.4 us
    all_gather x1, waiting for transfers between devices, on_device(): value_piece = lax.all_gather(value_rows, 'seq', axis=1, tiled=True)  64 us
    all_gather x1, waiting for transfers between devices, on_device(): lax.all_gather(conv_weight, 'batch', axis=2, tiled=True)  47.6 us
  transfers between devices with their start and end apart: 6, of which 4 were waited for; matrix products, arithmetic and copies ran while one was open for 4% of the time, Pallas kernels for 0%

commit v1 on v0

v1 whole, which is shorter than its diff:
```python
import functools

import jax
import jax.numpy as jnp
from jax import lax
from jax.experimental import pallas as pl
from jax.experimental.pallas import tpu as pltpu
from jax.sharding import PartitionSpec as P

HEADS = 8
KEY = 64
VAL = 96
epsilon = 1e-05

Y_LO, Z = 4, 8
Z_GROUPS = [[y * Z + z for z in range(Z)] for y in range(Y_LO)]
Y_GROUPS = [[y * Z + z for y in range(Y_LO)] for z in range(Z)]


def y_shift(step):
    pairs = []
    for batch in range(Y_LO * Z):
        for seq in range(16):
            y_lo, z = divmod(batch, Z)
            y_hi, rest = divmod(seq, 8)
            y = (y_hi * Y_LO + y_lo + step) % (2 * Y_LO)
            target = ((y % Y_LO) * Z + z) * 16 + (y // Y_LO) * 8 + rest
            pairs.append((batch * 16 + seq, target))
    return pairs


def y_lo_shift(step):
    return [(i, (i // Z + step) % Y_LO * Z + i % Z) for i in range(Y_LO * Z)]


def to_all(values, axis, groups=None):
    count = len(groups[0]) if groups else lax.axis_size(axis)
    return lax.all_to_all(
        jnp.broadcast_to(values[None], (count,) + values.shape),
        axis, 0, 0, axis_index_groups=groups, tiled=True,
    )


def attend_kernel(half_ref, r_ref, o_ref):
    first = half_ref[0] * 64
    keys = r_ref[:, :, :64].reshape(2048, KEY)
    values = r_ref[:, :, 128:224].reshape(2048, VAL)
    for i in range(4):
        q = r_ref[i * 4 : (i + 1) * 4, pl.ds(pl.multiple_of(first, 64), 64), 64:128]
        q = q.reshape(256, KEY)
        scores = lax.dot_general(
            q, keys, (((1,), (1,)), ((), ())), preferred_element_type=jnp.float32
        )
        exps = jnp.exp(scores - jnp.max(scores, axis=-1, keepdims=True))
        total = jnp.sum(exps, axis=-1, keepdims=True)
        out = jnp.dot(exps.astype(jnp.bfloat16), values, preferred_element_type=jnp.float32)
        out = (out / total).astype(jnp.bfloat16).reshape(4, 64, VAL)
        o_ref[i * 4 : (i + 1) * 4, :, :VAL] = out
        o_ref[i * 4 : (i + 1) * 4, :, VAL:] = jnp.zeros((4, 64, 128 - VAL), jnp.bfloat16)


def attend(half, received):
    return pl.pallas_call(
        attend_kernel,
        out_shape=jax.ShapeDtypeStruct((16, 64, 128), jnp.bfloat16),
        in_specs=[
            pl.BlockSpec(memory_space=pltpu.SMEM),
            pl.BlockSpec(memory_space=pltpu.VMEM),
        ],
        out_specs=pl.BlockSpec(memory_space=pltpu.VMEM),
        compiler_params=pltpu.CompilerParams(vmem_limit_bytes=40 << 20),
        name="attend",
    )(half, received)


def on_device(
    sequence_input, bn_gain, bn_bias, conv_weight, conv_bias, ln_gain, ln_bias, qkv_weight
):
    raw = sequence_input[0]
    channels = raw.shape[1]
    y_lo = lax.axis_index("batch") // Z
    seq = lax.axis_index("seq")
    core = seq % 2
    rel = (y_lo - jnp.arange(Y_LO)) % Y_LO

    both = jnp.concatenate(
        [conv_weight.transpose(0, 2, 1).reshape(120, channels), qkv_weight.T], axis=0
    )
    mine = lax.dynamic_slice(both, (0, core * 384), (176, 384))
    gathered = lax.all_gather(mine, "batch", axis=0, axis_index_groups=Z_GROUPS)
    swap = [(i, i ^ 1) for i in range(16)]
    conv_mine = gathered[:, :120]
    conv_other = lax.ppermute(conv_mine, "seq", swap)
    qkv_mine = gathered[:, 120:].reshape(448, 384)
    qkv_blocks = [qkv_mine] + [
        lax.ppermute(qkv_mine, ("batch", "seq"), y_shift(step)) for step in (1, 2, -1)
    ]
    qkv_mine = jnp.take(jnp.stack(qkv_blocks), rel, axis=0).reshape(1792, 384)
    qkv_other = lax.ppermute(qkv_mine, "seq", swap)

    def joined(own, other):
        low = jnp.where(core == 0, own, other)
        high = jnp.where(core == 0, other, own)
        return jnp.concatenate([low, high], axis=-1)

    blocks = jnp.stack(
        [raw] + [lax.ppermute(raw, "batch", y_lo_shift(k)) for k in range(1, Y_LO)]
    )

    wide = raw.astype(jnp.float32)
    sums = jnp.stack([jnp.sum(wide, axis=0), jnp.sum(wide * wide, axis=0)])
    edges = jnp.concatenate([wide[:2], wide[-2:]], axis=0)
    first = to_all(jnp.concatenate([sums, edges], axis=0), "seq")
    sums = jnp.sum(first[:, :2], axis=0)
    left = lax.dynamic_index_in_dim(first, jnp.maximum(seq - 1, 0), 0, keepdims=False)[4:6]
    right = lax.dynamic_index_in_dim(first, jnp.minimum(seq + 1, 15), 0, keepdims=False)[2:4]
    sums = jnp.sum(to_all(sums, "batch", Z_GROUPS), axis=0)
    third = to_all(jnp.concatenate([sums, left, right], axis=0), "batch", Y_GROUPS)
    sums = jnp.sum(third[:, :2], axis=0)
    halos = jnp.take(third[:, 2:], rel, axis=0)
    count = float(raw.shape[0] * lax.axis_size("batch") * lax.axis_size("seq"))
    mean = sums[0] / count
    var = sums[1] / count - mean * mean

    def activate(values):
        return jax.nn.gelu(
            (values - mean) * lax.rsqrt(var + epsilon) * bn_gain + bn_bias, approximate=True
        ).astype(jnp.bfloat16)

    left = jnp.where(seq > 0, activate(halos[:, :2]), 0)
    right = jnp.where(seq < 15, activate(halos[:, 2:]), 0)
    rows = jnp.concatenate([left, activate(blocks.astype(jnp.float32)), right], axis=1)

    kernel = joined(conv_mine, conv_other).reshape(Z, 5, 24, channels)
    kernel = kernel.transpose(1, 0, 2, 3).reshape(5, 192, channels)
    conv = None
    for tap in range(5):
        product = jnp.einsum(
            "kpc,oc->kpo", rows[:, tap : tap + 256], kernel[tap],
            preferred_element_type=jnp.float32,
        )
        conv = product if conv is None else conv + product
    conv = conv + lax.dynamic_slice(conv_bias, (y_lo * 192,), (192,))
    part = conv.reshape(Y_LO, 128, 2, 192).max(axis=2).astype(jnp.bfloat16)
    part = lax.all_to_all(
        jnp.take(part, rel, axis=0), "batch", 0, 0, axis_index_groups=Y_GROUPS, tiled=True
    )
    pooled = part.transpose(1, 0, 2).reshape(128, channels)

    pooled_wide = pooled.astype(jnp.float32)
    centre = jnp.mean(pooled_wide, axis=-1, keepdims=True)
    spread = jnp.mean((pooled_wide - centre) ** 2, axis=-1, keepdims=True)
    normed = ((pooled_wide - centre) * lax.rsqrt(spread + epsilon) * ln_gain + ln_bias).astype(
        jnp.bfloat16
    )
    proj = jnp.einsum(
        "bd,kd->bk", normed, joined(qkv_mine, qkv_other), preferred_element_type=jnp.float32
    )
    queries = (proj[:, :512] * KEY ** (-0.5)).astype(jnp.bfloat16).reshape(128, HEADS, KEY)
    keys = proj[:, 512:1024].astype(jnp.bfloat16).reshape(128, HEADS, KEY)
    values = proj[:, 1024:].astype(jnp.bfloat16).reshape(128, HEADS, VAL)
    pad = jnp.zeros((128, HEADS, 32), jnp.bfloat16)
    packed = jnp.concatenate([keys, queries, values, pad], axis=-1).transpose(1, 0, 2)
    packed = jnp.broadcast_to(packed[None], (2,) + packed.shape).reshape(16, 128, 256)
    received = lax.all_to_all(packed, "seq", 0, 0, tiled=True)
    out = attend((seq // 8).astype(jnp.int32)[None], received)
    out = lax.all_to_all(out, "seq", 0, 0, tiled=True)[..., :VAL]
    attended = out.reshape(2, HEADS, 64, VAL).transpose(0, 2, 1, 3).reshape(128, HEADS * VAL)
    return (pooled[None], attended[None])


def solution(mesh):
    placed = (
        P("batch", "seq", None),
        P(),
        P(),
        P(None, None, "batch"),
        P(),
        P(),
        P(),
        P(None, "batch"),
    )
    return jax.shard_map(
        on_device,
        mesh=mesh,
        in_specs=placed,
        out_specs=(P("batch", "seq", None), P("batch", "seq", None)),
        check_vma=False,
    )
```

time: 495 us -> 204 us (0.41)
  waiting for transfers between devices: 330 us -> 85.8 us
  blocking collectives: 110 us -> 0 us
  starting transfers between devices: 3.28 us -> 66.7 us
  matrix products: 17.6 us -> 4.48 us
  other arithmetic: 6.26 us -> 12 us
    all_gather x4 -> x1, waiting for transfers between devices: 329 us -> 0.02 us  [on_device(): gathered = lax.all_gather(mine, 'batch', axis=0, axis_index_groups=Z_GROUPS)]
    psum x1 -> x0, blocking collectives: 110 us -> none  [on_device(): lax.psum((jnp.sum(values_in, axis=(0, 1)), jnp.sum(values_in * values_in,...]
    all_to_all x0 -> x6, waiting for transfers between devices: none -> 65.2 us  [the longest x1 31.4 us: on_device(): received = lax.all_to_all(packed, 'seq', 0, 0, tiled=True)]
    all_to_all x0 -> x6, starting transfers between devices: none -> 43.9 us  [the longest x3 31.4 us: to_all(): lax.all_to_all(jnp.broadcast_to(values[None], (count,) + values.shape), a...]
    ppermute x2 -> x8, waiting for transfers between devices: 0.01 us -> 20.6 us  [the longest x3 20.6 us: on_device(): lax.ppermute(qkv_mine, ('batch', 'seq'), y_shift(step))]
    ppermute x2 -> x8, starting transfers between devices: 2.95 us -> 22.7 us  [the longest x3 9.49 us: on_device(): lax.ppermute(qkv_mine, ('batch', 'seq'), y_shift(step))]
    dot_general x14 -> x6, matrix products: 17.6 us -> 4.48 us  [the longest x5 3.45 us: on_device(): jnp.einsum('kpc,oc->kpo', rows[:, tap:tap + 256], kernel[tap], preferred_...]
    all_gather x2 -> x0, local copies, waits for them, and re-layouts: 7.63 us -> none  [the longest x1 4.71 us: on_device(): value_piece = lax.all_gather(value_rows, 'seq', axis=1, tiled=True)]
  transfers between devices with their start and end apart: 6 -> 15, of which waited for: 4 -> 9; matrix products, arithmetic and copies ran while one was open for 4% -> 8% of each run, Pallas kernels for 0% -> 0%
where the time goes in v1:
time: 204 us; the launch traced here: 203 us
  waiting for transfers between devices  85.8 us (42%)
  starting transfers between devices  66.7 us (33%)
  local copies, waits for them, and re-layouts  15 us (7%)
  between operations  14.6 us (7%)
  other arithmetic  12 us (6%)
  matrix products  4.48 us (2%)
  Pallas kernels  4.11 us (2%)
    all_to_all x1, waiting for transfers between devices, on_device(): received = lax.all_to_all(packed, 'seq', 0, 0, tiled=True)  31.4 us
    all_to_all x3, starting transfers between devices, to_all(): lax.all_to_all(jnp.broadcast_to(values[None], (count,) + values.shape), a...  31.4 us
    ppermute x3, waiting for transfers between devices, on_device(): lax.ppermute(qkv_mine, ('batch', 'seq'), y_shift(step))  20.6 us
    all_to_all x3, waiting for transfers between devices, to_all(): lax.all_to_all(jnp.broadcast_to(values[None], (count,) + values.shape), a...  19.3 us
    all_to_all x1, waiting for transfers between devices, on_device(): out = lax.all_to_all(out, 'seq', 0, 0, tiled=True)[..., :VAL]  11.8 us
    ppermute x3, starting transfers between devices, on_device(): lax.ppermute(qkv_mine, ('batch', 'seq'), y_shift(step))  9.49 us
    ppermute x3, starting transfers between devices, on_device(): lax.ppermute(raw, 'batch', y_lo_shift(k))  9.44 us
    all_to_all x1, starting transfers between devices, on_device(): lax.all_to_all(jnp.take(part, rel, axis=0), 'batch', 0, 0, axis_index_gro...  5.16 us
  transfers between devices with their start and end apart: 15, of which 9 were waited for; matrix products, arithmetic and copies ran while one was open for 8% of the time, Pallas kernels for 0%

profile of v1, /device:TPU:8, one launch (start us, length us, event | category | flops | bytes accessed | tf_op | source)
XLA Modules:
  0.0 202.7 jit_solution(14549519566475244030)
XLA Ops:
  10.9 8.9 %all-to-all-start = ((f32[16,6,768]{2,1,0:T(8,128)}), f32[16,6,768]{2,1,0:T(8,128)S(1)}, u32[]{:S(2)}, u32[]{:S(2)}) async-start(f32[16,6,768]{2,1,0:T(8,128)} %broadcast_in_dim.53), calls=%async_computation | async-start | bytes 786432 | tf_op jit(solution)/shard_map/all_to_all | solution.py:38
  19.8 3.3 %collective-permute-start.2 = (bf16[256,768]{1,0:T(8,128)(2,1)S(1)}, bf16[256,768]{1,0:T(8,128)(2,1)S(1)}, u32[]{:S(2)}, u32[]{:S(2)}) collective-permute-start(bf16[256,768]{1,0:T(8,128)(2,1)S(1)} %bitcast.87), channel_id=1, source_target_pairs={{0,384},{16,400},{32,416},{48,432},{64,448},{80,464},{96,480},{112... | collective-permute-start | bytes 1179656 | tf_op jit(solution)/shard_map/ppermute | solution.py:107
  23.1 2.7 %collective-permute-start.1 = (bf16[256,768]{1,0:T(8,128)(2,1)S(1)}, bf16[256,768]{1,0:T(8,128)(2,1)S(1)}, u32[]{:S(2)}, u32[]{:S(2)}) collective-permute-start(bf16[256,768]{1,0:T(8,128)(2,1)S(1)} %bitcast.88), channel_id=1, source_target_pairs={{0,256},{16,272},{32,288},{48,304},{64,320},{80,336},{96,352},{112... | collective-permute-start | bytes 1179656 | tf_op jit(solution)/shard_map/ppermute | solution.py:107
  25.8 3.5 %collective-permute-start = (bf16[256,768]{1,0:T(8,128)(2,1)S(1)}, bf16[256,768]{1,0:T(8,128)(2,1)S(1)}, u32[]{:S(2)}, u32[]{:S(2)}) collective-permute-start(bf16[256,768]{1,0:T(8,128)(2,1)S(1)} %bitcast.89), channel_id=1, source_target_pairs={{0,128},{16,144},{32,160},{48,176},{64,192},{80,208},{96,224},{112... | collective-permute-start | bytes 1179656 | tf_op jit(solution)/shard_map/ppermute | solution.py:107
  31.4 6.2 %all-to-all-done = f32[16,6,768]{2,1,0:T(8,128)S(1)} async-done(((f32[16,6,768]{2,1,0:T(8,128)}), f32[16,6,768]{2,1,0:T(8,128)S(1)}, u32[]{:S(2)}, u32[]{:S(2)}) %all-to-all-start) | async-done | bytes 294944 | tf_op jit(solution)/shard_map/all_to_all | solution.py:38
  38.4 10.3 %all-to-all-start.1 = ((f32[8,2,768]{2,1,0:T(2,128)}), f32[8,2,768]{2,1,0:T(2,128)S(1)}, u32[]{:S(2)}, u32[]{:S(2)}) async-start(f32[8,2,768]{2,1,0:T(2,128)} %broadcast_in_dim.54), calls=%async_computation.1 | async-start | bytes 98304 | tf_op jit(solution)/shard_map/all_to_all | solution.py:38
  48.7 8.2 %all-to-all-done.1 = f32[8,2,768]{2,1,0:T(2,128)S(1)} async-done(((f32[8,2,768]{2,1,0:T(2,128)}), f32[8,2,768]{2,1,0:T(2,128)S(1)}, u32[]{:S(2)}, u32[]{:S(2)}) %all-to-all-start.1) | async-done | bytes 49184 | tf_op jit(solution)/shard_map/all_to_all | solution.py:38
  57.6 12.1 %all-to-all-start.2 = ((f32[4,6,768]{2,1,0:T(8,128)}), f32[4,6,768]{2,1,0:T(8,128)S(1)}, u32[]{:S(2)}, u32[]{:S(2)}) async-start(f32[4,6,768]{2,1,0:T(8,128)} %broadcast_in_dim.90), calls=%async_computation.2 | async-start | bytes 196608 | tf_op jit(solution)/shard_map/all_to_all | solution.py:38
  69.7 4.9 %all-to-all-done.2 = f32[4,6,768]{2,1,0:T(8,128)S(1)} async-done(((f32[4,6,768]{2,1,0:T(8,128)}), f32[4,6,768]{2,1,0:T(8,128)S(1)}, u32[]{:S(2)}, u32[]{:S(2)}) %all-to-all-start.2) | async-done | bytes 73760 | tf_op jit(solution)/shard_map/all_to_all | solution.py:38
  74.7 2.1 %slice.139 = bf16[8,120,384]{2,1,0:T(8,128)(2,1)} slice(bf16[8,176,384]{2,1,0:T(8,128)(2,1)} %bitcast.90), slice={[0:8], [0:120], [0:384]} | slice | bytes 1474560 | tf_op jit(solution)/shard_map/slice | solution.py:92
  82.0 2.8 %collective-permute-start.6 = (bf16[448,384]{1,0:T(8,128)(2,1)S(1)}, bf16[448,384]{1,0:T(8,128)(2,1)S(1)}, u32[]{:S(2)}, u32[]{:S(2)}) collective-permute-start(bf16[448,384]{1,0:T(8,128)(2,1)S(1)} %bitcast.93), channel_id=1, source_target_pairs={{0,392},{1,393},{2,394},{3,395},{4,396},{5,397},{6,398},{7,399},{8... | collective-permute-start | bytes 1032200 | tf_op jit(solution)/shard_map/ppermute | solution.py:96
  84.8 2.7 %collective-permute-start.5 = (bf16[448,384]{1,0:T(8,128)(2,1)S(1)}, bf16[448,384]{1,0:T(8,128)(2,1)S(1)}, u32[]{:S(2)}, u32[]{:S(2)}) collective-permute-start(bf16[448,384]{1,0:T(8,128)(2,1)S(1)} %bitcast.94), channel_id=1, source_target_pairs={{0,256},{1,257},{2,258},{3,259},{4,260},{5,261},{6,262},{7,263},{8... | collective-permute-start | bytes 1032200 | tf_op jit(solution)/shard_map/ppermute | solution.py:96
  87.6 3.9 %collective-permute-start.4 = (bf16[448,384]{1,0:T(8,128)(2,1)S(1)}, bf16[448,384]{1,0:T(8,128)(2,1)S(1)}, u32[]{:S(2)}, u32[]{:S(2)}) collective-permute-start(bf16[448,384]{1,0:T(8,128)(2,1)S(1)} %bitcast.95), channel_id=1, source_target_pairs={{0,128},{1,129},{2,130},{3,131},{4,132},{5,133},{6,134},{7,135},{8... | collective-permute-start | bytes 1032200 | tf_op jit(solution)/shard_map/ppermute | solution.py:96
  91.7 2.6 %collective-permute-done.6 = bf16[448,384]{1,0:T(8,128)(2,1)S(1)} collective-permute-done((bf16[448,384]{1,0:T(8,128)(2,1)S(1)}, bf16[448,384]{1,0:T(8,128)(2,1)S(1)}, u32[]{:S(2)}, u32[]{:S(2)}) %collective-permute-start.6) | collective-permute-done | bytes 344096 | tf_op jit(solution)/shard_map/ppermute | solution.py:96
  94.3 12.2 %collective-permute-done.5 = bf16[448,384]{1,0:T(8,128)(2,1)S(1)} collective-permute-done((bf16[448,384]{1,0:T(8,128)(2,1)S(1)}, bf16[448,384]{1,0:T(8,128)(2,1)S(1)}, u32[]{:S(2)}, u32[]{:S(2)}) %collective-permute-start.5) | collective-permute-done | bytes 344096 | tf_op jit(solution)/shard_map/ppermute | solution.py:96
  106.6 5.7 %collective-permute-done.4 = bf16[448,384]{1,0:T(8,128)(2,1)S(1)} collective-permute-done((bf16[448,384]{1,0:T(8,128)(2,1)S(1)}, bf16[448,384]{1,0:T(8,128)(2,1)S(1)}, u32[]{:S(2)}, u32[]{:S(2)}) %collective-permute-start.4) | collective-permute-done | bytes 344096 | tf_op jit(solution)/shard_map/ppermute | solution.py:96
  113.6 2.2 %gather_fusion.2 = bf16[4,448,384]{2,1,0:T(8,128)(2,1)S(1)} fusion(bf16[4,448,384]{2,1,0:T(8,128)(2,1)} %pad_maximum_fusion.5, s32[1024]{0:T(1024)S(1)} %pad_clamp_fusion), kind=kCustom, calls=%fused_computation.2 | custom fusion | bytes 2752528 | tf_op jit(solution)/shard_map/jit(_take)/gather | solution.py:98
  123.3 5.2 %all-to-all-start.3 = ((bf16[4,128,192]{1,2,0:T(8,128)(2,1)}), bf16[4,128,192]{1,2,0:T(8,128)(2,1)S(1)}, u32[]{:S(2)}, u32[]{:S(2)}) async-start(bf16[4,128,192]{1,2,0:T(8,128)(2,1)} %broadcast_select_fusion.4), calls=%async_computation.3 | async-start | bytes 393216 | tf_op jit(solution)/shard_map/all_to_all | solution.py:145
  131.9 2.7 %all-to-all-done.3 = bf16[4,128,192]{1,2,0:T(8,128)(2,1)S(1)} async-done(((bf16[4,128,192]{1,2,0:T(8,128)(2,1)}), bf16[4,128,192]{1,2,0:T(8,128)(2,1)S(1)}, u32[]{:S(2)}, u32[]{:S(2)}) %all-to-all-start.3) | async-done | bytes 196640 | tf_op jit(solution)/shard_map/all_to_all | solution.py:145
  139.2 3.8 %all-to-all-start.4 = ((bf16[16,128,256]{2,1,0:T(8,128)(2,1)}), bf16[16,128,256]{2,1,0:T(8,128)(2,1)S(1)}, u32[]{:S(2)}, u32[]{:S(2)}) async-start(bf16[16,128,256]{2,1,0:T(8,128)(2,1)} %bitcast.39), calls=%async_computation.4 | async-start | bytes 2097152 | tf_op jit(solution)/shard_map/all_to_all | solution.py:165
  143.1 31.4 %all-to-all-done.4.r_ref = bf16[16,128,256]{2,1,0:T(8,128)(2,1)S(1)} async-done(((bf16[16,128,256]{2,1,0:T(8,128)(2,1)}), bf16[16,128,256]{2,1,0:T(8,128)(2,1)S(1)}, u32[]{:S(2)}, u32[]{:S(2)}) %all-to-all-start.4) | async-done | bytes 1048608 | tf_op jit(solution)/shard_map/all_to_all | solution.py:165
  174.5 4.1 %attend.1 = bf16[16,64,128]{2,1,0:T(8,128)(2,1)} custom-call(s32[1]{0:T(128)} %bitcast.27.half_ref, bf16[16,128,256]{2,1,0:T(8,128)(2,1)S(1)} %all-to-all-done.4.r_ref), custom_call_target="tpu_custom_call" | custom-call | tf_op jit(solution)/shard_map/attend/pallas_call | solution.py:63
  178.6 3.5 %all-to-all-start.5 = ((bf16[16,64,128]{2,1,0:T(8,128)(2,1)}), bf16[16,64,128]{2,1,0:T(8,128)(2,1)S(1)}, u32[]{:S(2)}, u32[]{:S(2)}) async-start(bf16[16,64,128]{2,1,0:T(8,128)(2,1)} %attend.1), calls=%async_computation.5 | async-start | bytes 524288 | tf_op jit(solution)/shard_map/all_to_all | solution.py:167
  182.9 11.8 %all-to-all-done.5 = bf16[16,64,128]{2,1,0:T(8,128)(2,1)S(1)} async-done(((bf16[16,64,128]{2,1,0:T(8,128)(2,1)}), bf16[16,64,128]{2,1,0:T(8,128)(2,1)S(1)}, u32[]{:S(2)}, u32[]{:S(2)}) %all-to-all-start.5) | async-done | bytes 262176 | tf_op jit(solution)/shard_map/all_to_all | solution.py:167
  (94 shorter events, 31.1 us)
Async XLA Ops:
  7.2 2.8 %copy-start = (bf16[1,256,768]{2,1,0:T(8,128)(2,1)S(1)}, bf16[1,256,768]{2,1,0:T(8,128)(2,1)}, u32[]{:S(2)}) copy-start(bf16[1,256,768]{2,1,0:T(8,128)(2,1)} %param.8) | copy-start | bytes 1179652
  7.2 67.5 %all-gather.3.cloned.1.call-start = ((), (), s32[]{:S(2)}) async-start(), calls=%async_computation.6 | async-start | bytes 1216512 | tf_op jit(solution)/shard_map/all_gather | solution.py:90
  10.9 67.8 %copy-start.1 = (f32[768]{0:T(1024)S(1)}, f32[768]{0:T(1024)}, u32[]{:S(2)}) copy-start(f32[768]{0:T(1024)} %param.10) | copy-start | bytes 9220
  10.9 67.9 %copy-start.2 = (f32[768]{0:T(1024)S(1)}, f32[768]{0:T(1024)}, u32[]{:S(2)}) copy-start(f32[768]{0:T(1024)} %param.9) | copy-start | bytes 9220
  10.9 26.8 %all-to-all-start = ((f32[16,6,768]{2,1,0:T(8,128)}), f32[16,6,768]{2,1,0:T(8,128)S(1)}, u32[]{:S(2)}, u32[]{:S(2)}) async-start(f32[16,6,768]{2,1,0:T(8,128)} %broadcast_in_dim.53), calls=%async_computation | async-start | bytes 786432 | tf_op jit(solution)/shard_map/all_to_all | solution.py:38
  19.8 58.9 %collective-permute-start.2 = (bf16[256,768]{1,0:T(8,128)(2,1)S(1)}, bf16[256,768]{1,0:T(8,128)(2,1)S(1)}, u32[]{:S(2)}, u32[]{:S(2)}) collective-permute-start(bf16[256,768]{1,0:T(8,128)(2,1)S(1)} %bitcast.87), channel_id=1, source_target_pairs={{0,384},{16,400},{32,416},{48,432},{64,448},{80,464},{96,480},{112... | collective-permute-start | bytes 1179656 | tf_op jit(solution)/shard_map/ppermute | solution.py:107
  23.1 55.7 %collective-permute-start.1 = (bf16[256,768]{1,0:T(8,128)(2,1)S(1)}, bf16[256,768]{1,0:T(8,128)(2,1)S(1)}, u32[]{:S(2)}, u32[]{:S(2)}) collective-permute-start(bf16[256,768]{1,0:T(8,128)(2,1)S(1)} %bitcast.88), channel_id=1, source_target_pairs={{0,256},{16,272},{32,288},{48,304},{64,320},{80,336},{96,352},{112... | collective-permute-start | bytes 1179656 | tf_op jit(solution)/shard_map/ppermute | solution.py:107
  25.8 53.0 %collective-permute-start = (bf16[256,768]{1,0:T(8,128)(2,1)S(1)}, bf16[256,768]{1,0:T(8,128)(2,1)S(1)}, u32[]{:S(2)}, u32[]{:S(2)}) collective-permute-start(bf16[256,768]{1,0:T(8,128)(2,1)S(1)} %bitcast.89), channel_id=1, source_target_pairs={{0,128},{16,144},{32,160},{48,176},{64,192},{80,208},{96,224},{112... | collective-permute-start | bytes 1179656 | tf_op jit(solution)/shard_map/ppermute | solution.py:107
  29.3 0.6 copy-start.3
  38.4 18.5 %all-to-all-start.1 = ((f32[8,2,768]{2,1,0:T(2,128)}), f32[8,2,768]{2,1,0:T(2,128)S(1)}, u32[]{:S(2)}, u32[]{:S(2)}) async-start(f32[8,2,768]{2,1,0:T(2,128)} %broadcast_in_dim.54), calls=%async_computation.1 | async-start | bytes 98304 | tf_op jit(solution)/shard_map/all_to_all | solution.py:38
  57.6 17.0 %all-to-all-start.2 = ((f32[4,6,768]{2,1,0:T(8,128)}), f32[4,6,768]{2,1,0:T(8,128)S(1)}, u32[]{:S(2)}, u32[]{:S(2)}) async-start(f32[4,6,768]{2,1,0:T(8,128)} %broadcast_in_dim.90), calls=%async_computation.2 | async-start | bytes 196608 | tf_op jit(solution)/shard_map/all_to_all | solution.py:38
  76.8 39.0 %collective-permute-start.3 = (bf16[8,120,384]{2,1,0:T(8,128)(2,1)}, bf16[8,120,384]{2,1,0:T(8,128)(2,1)}, u32[]{:S(2)}, u32[]{:S(2)}) collective-permute-start(bf16[8,120,384]{2,1,0:T(8,128)(2,1)} %slice.139), channel_id=1, source_target_pairs={{0,1},{1,0},{2,3},{3,2},{4,5},{5,4},{6,7},{7,6},{8,9},{9,8},{10,11... | collective-permute-start | bytes 2211848 | tf_op jit(solution)/shard_map/ppermute | solution.py:93
  78.8 12.7 %copy-start.4 = (pred[4]{0:T(512)(128)(4,1)S(1)}, pred[4]{0:T(512)(128)(4,1)}, u32[]{:S(2)}) copy-start(pred[4]{0:T(512)(128)(4,1)} %copy-done.3) | copy-start | bytes 16
  82.0 12.4 %collective-permute-start.6 = (bf16[448,384]{1,0:T(8,128)(2,1)S(1)}, bf16[448,384]{1,0:T(8,128)(2,1)S(1)}, u32[]{:S(2)}, u32[]{:S(2)}) collective-permute-start(bf16[448,384]{1,0:T(8,128)(2,1)S(1)} %bitcast.93), channel_id=1, source_target_pairs={{0,392},{1,393},{2,394},{3,395},{4,396},{5,397},{6,398},{7,399},{8... | collective-permute-start | bytes 1032200 | tf_op jit(solution)/shard_map/ppermute | solution.py:96
  84.8 21.7 %collective-permute-start.5 = (bf16[448,384]{1,0:T(8,128)(2,1)S(1)}, bf16[448,384]{1,0:T(8,128)(2,1)S(1)}, u32[]{:S(2)}, u32[]{:S(2)}) collective-permute-start(bf16[448,384]{1,0:T(8,128)(2,1)S(1)} %bitcast.94), channel_id=1, source_target_pairs={{0,256},{1,257},{2,258},{3,259},{4,260},{5,261},{6,262},{7,263},{8... | collective-permute-start | bytes 1032200 | tf_op jit(solution)/shard_map/ppermute | solution.py:96
  87.6 24.7 %collective-permute-start.4 = (bf16[448,384]{1,0:T(8,128)(2,1)S(1)}, bf16[448,384]{1,0:T(8,128)(2,1)S(1)}, u32[]{:S(2)}, u32[]{:S(2)}) collective-permute-start(bf16[448,384]{1,0:T(8,128)(2,1)S(1)} %bitcast.95), channel_id=1, source_target_pairs={{0,128},{1,129},{2,130},{3,131},{4,132},{5,133},{6,134},{7,135},{8... | collective-permute-start | bytes 1032200 | tf_op jit(solution)/shard_map/ppermute | solution.py:96
  119.5 0.7 copy-start.8
  121.0 1.5 copy-start.5
  123.3 11.3 %all-to-all-start.3 = ((bf16[4,128,192]{1,2,0:T(8,128)(2,1)}), bf16[4,128,192]{1,2,0:T(8,128)(2,1)S(1)}, u32[]{:S(2)}, u32[]{:S(2)}) async-start(bf16[4,128,192]{1,2,0:T(8,128)(2,1)} %broadcast_select_fusion.4), calls=%async_computation.3 | async-start | bytes 393216 | tf_op jit(solution)/shard_map/all_to_all | solution.py:145
  128.5 6.4 %copy-start.6 = (f32[768]{0:T(1024)S(1)}, f32[768]{0:T(1024)}, u32[]{:S(2)}) copy-start(f32[768]{0:T(1024)} %param.14) | copy-start | bytes 9220
  128.5 6.4 %copy-start.7 = (f32[768]{0:T(1024)S(1)}, f32[768]{0:T(1024)}, u32[]{:S(2)}) copy-start(f32[768]{0:T(1024)} %param.13) | copy-start | bytes 9220
  129.9 5.2 %collective-permute-start.7 = (bf16[1792,384]{1,0:T(8,128)(2,1)}, bf16[1792,384]{1,0:T(8,128)(2,1)S(1)}, u32[]{:S(2)}, u32[]{:S(2)}) collective-permute-start(bf16[1792,384]{1,0:T(8,128)(2,1)} %bitcast_select_fusion), channel_id=1, source_target_pairs={{0,1},{1,0},{2,3},{3,2},{4,5},{5,4},{6,7},{7,6},{8,9},{9,8},{10,11... | collective-permute-start | bytes 4128776 | tf_op jit(solution)/shard_map/ppermute | solution.py:99
  139.2 35.2 %all-to-all-start.4 = ((bf16[16,128,256]{2,1,0:T(8,128)(2,1)}), bf16[16,128,256]{2,1,0:T(8,128)(2,1)S(1)}, u32[]{:S(2)}, u32[]{:S(2)}) async-start(bf16[16,128,256]{2,1,0:T(8,128)(2,1)} %bitcast.39), calls=%async_computation.4 | async-start | bytes 2097152 | tf_op jit(solution)/shard_map/all_to_all | solution.py:165
  178.6 16.2 %all-to-all-start.5 = ((bf16[16,64,128]{2,1,0:T(8,128)(2,1)}), bf16[16,64,128]{2,1,0:T(8,128)(2,1)S(1)}, u32[]{:S(2)}, u32[]{:S(2)}) async-start(bf16[16,64,128]{2,1,0:T(8,128)(2,1)} %attend.1), calls=%async_computation.5 | async-start | bytes 524288 | tf_op jit(solution)/shard_map/all_to_all | solution.py:167
Sparse Core Ops, SparseCore 0:
  10.7 46.7 all-gather.2

commit v2 on v1

v2 whole, which is shorter than its diff:
```python
import functools

import jax
import jax.numpy as jnp
from jax import lax
from jax.experimental import pallas as pl
from jax.experimental.pallas import tpu as pltpu
from jax.sharding import PartitionSpec as P

HEADS = 8
KEY = 64
VAL = 96
ROWS = 2 * KEY + VAL
epsilon = 1e-05

Y_LO, Z = 4, 8
Z_GROUPS = [[y * Z + z for z in range(Z)] for y in range(Y_LO)]
X_GROUPS = [[half * 8 + x * 2 + core for x in range(4)] for half in range(2) for core in range(2)]
HALF_GROUPS = [list(range(8)), list(range(8, 16))]


def x_shift(step):
    return [(i, i // 8 * 8 + (i // 2 + step) % 4 * 2 + i % 2) for i in range(16)]


def quarters():
    pairs = []
    for batch in range(Y_LO * Z):
        for seq in range(16):
            y_lo, z = divmod(batch, Z)
            y_hi, x = seq // 8, seq // 2 % 4
            source = (y_hi * Y_LO + y_lo + (0, 1, 2, -1)[x]) % (2 * Y_LO)
            source_batch = source % Y_LO * Z + z
            pairs.append((source_batch * 16 + source // Y_LO * 8 + seq % 8, batch * 16 + seq))
    return pairs


def to_all(values, axis, groups=None):
    count = len(groups[0]) if groups else lax.axis_size(axis)
    return lax.all_to_all(
        jnp.broadcast_to(values[None], (count,) + values.shape),
        axis, 0, 0, axis_index_groups=groups, tiled=True,
    )


def qkv_rows(gathered):
    tiles = gathered[:, :, 1920:].reshape(Z, 3, 8, 7, 128)
    return tiles.transpose(0, 3, 2, 1, 4).reshape(448, 384)


def attend_kernel(first_ref, r_ref, o_ref):
    keys = jnp.concatenate([r_ref[j, KEY : 2 * KEY, :] for j in range(16)], axis=1).T
    values = jnp.concatenate([r_ref[j, 2 * KEY :, :] for j in range(16)], axis=1)
    first = first_ref[0]
    for i in range(0, 8, 2):
        q = jnp.concatenate([r_ref[first + i, :KEY, :], r_ref[first + i + 1, :KEY, :]], axis=1)
        scores = jnp.dot(keys, q, preferred_element_type=jnp.float32)
        exps = jnp.exp(scores - jnp.max(scores, axis=0, keepdims=True))
        total = jnp.sum(exps, axis=0, keepdims=True)
        out = jnp.dot(values, exps.astype(jnp.bfloat16), preferred_element_type=jnp.float32)
        out = (out / total).astype(jnp.bfloat16)
        o_ref[i] = out[:, :128]
        o_ref[i + 1] = out[:, 128:]


def attend(first, received):
    return pl.pallas_call(
        attend_kernel,
        out_shape=jax.ShapeDtypeStruct((8, VAL, 128), jnp.bfloat16),
        in_specs=[
            pl.BlockSpec(memory_space=pltpu.SMEM),
            pl.BlockSpec(memory_space=pltpu.VMEM),
        ],
        out_specs=pl.BlockSpec(memory_space=pltpu.VMEM),
        compiler_params=pltpu.CompilerParams(vmem_limit_bytes=20 << 20),
        name="attend",
    )(first, received)


def conv_kernel(where_ref, x0, x1, x2, x3, sums_ref, norm_ref, mine_ref, other_ref, bias_ref,
                out_ref, act, product, held, arrived, *, count):
    core, x_at, y_hi = where_ref[0], where_ref[1], where_ref[2]
    mean = sums_ref[0:1] / count
    scale = lax.rsqrt(sums_ref[1:2] / count - mean * mean + epsilon) * norm_ref[0:1]
    shift = norm_ref[1:2]
    near = pl.multiple_of(core * 384, 128)
    far = pl.multiple_of(384 - core * 384, 128)

    def activated(values):
        return jax.nn.gelu(
            (values.astype(jnp.float32) - mean) * scale + shift, approximate=True
        ).astype(jnp.bfloat16)

    copies = [
        pltpu.make_async_copy(x_ref, held.at[k], arrived.at[k])
        for k, x_ref in enumerate((x0, x1, x2, x3))
    ]
    for copy in copies:
        copy.start()
    for k in range(4):
        copies[k].wait()
        slot = lax.rem(x_at + 4 - k, 4)
        seq = y_hi * 8 + slot * 2 + core
        edge = activated(held[k, 0:16])
        row = lax.broadcasted_iota(jnp.int32, edge.shape, 0)
        act[k, 0:16] = jnp.where((row >= 14) & (seq > 0), edge, jnp.zeros_like(edge))
        edge = activated(held[k, 272:288])
        act[k, 272:288] = jnp.where((row < 2) & (seq < 15), edge, jnp.zeros_like(edge))

        @pl.loop(1, 17)
        def _(i):
            rows = pl.ds(pl.multiple_of(i * 16, 16), 16)
            act[k, rows] = activated(held[k, rows])

        for tap in range(5):
            nt = (((1,), (1,)), ((), ()))
            both = lax.dot_general(
                act[k, :, pl.ds(near, 384)], mine_ref[:, tap * 384 : (tap + 1) * 384], nt, preferred_element_type=jnp.float32
            ) + lax.dot_general(
                act[k, :, pl.ds(far, 384)], other_ref[:, tap * 384 : (tap + 1) * 384], nt, preferred_element_type=jnp.float32
            )
            product[tap] = both[:, :128]
            product[5 + tap, :, :64] = both[:, 128:]
        for base, lanes in ((0, 128), (5, 64)):
            pair = []
            for odd in range(2):
                total = product[base, pl.ds(14 + odd, 128, stride=2), :]
                for tap in range(1, 5):
                    total = total + product[base + tap, pl.ds(14 + odd + tap, 128, stride=2), :]
                pair.append(total[:, :lanes])
            columns = slice(base // 5 * 128, base // 5 * 128 + lanes)
            pooled = jnp.maximum(pair[0], pair[1]) + bias_ref[:, columns]
            pooled = pooled.astype(jnp.bfloat16)
            if base == 0:
                out_ref[slot, :128] = pooled
            else:
                out_ref[slot, 128:, :64] = pooled[:64]
                out_ref[slot, 128:, 64:] = pooled[64:]


def conv_block(where, blocks, sums, norm, mine, other, bias, count):
    vmem = pl.BlockSpec(memory_space=pltpu.VMEM)
    return pl.pallas_call(
        functools.partial(conv_kernel, count=count),
        out_shape=jax.ShapeDtypeStruct((4, 192, 128), jnp.bfloat16),
        in_specs=[pl.BlockSpec(memory_space=pltpu.SMEM)]
        + [pl.BlockSpec(memory_space=pl.ANY)] * 4
        + [vmem] * 5,
        out_specs=vmem,
        scratch_shapes=[
            pltpu.VMEM((4, 288, 768), jnp.bfloat16),
            pltpu.VMEM((10, 288, 128), jnp.float32),
            pltpu.VMEM((4, 288, 768), jnp.bfloat16),
            pltpu.SemaphoreType.DMA((4,)),
        ],
        compiler_params=pltpu.CompilerParams(vmem_limit_bytes=14 << 20),
        name="conv_block",
    )(where, *blocks, sums, norm, mine, other, bias)


def project_kernel(where_ref, part_ref, norm_ref, *refs):
    weights, (pooled_ref, out_ref, normed, proj) = refs[:8], refs[8:]
    core, x_at, y_lo = where_ref[0], where_ref[1], where_ref[3]
    near = pl.multiple_of(core * 384, 128)
    far = pl.multiple_of(384 - core * 384, 128)
    pieces = []
    for i in range(4):
        piece = part_ref[lax.rem(i + 4 - y_lo, 4)]
        pieces.append(piece[:128])
        pieces.append(jnp.concatenate([piece[128:, :64], piece[128:, 64:]], axis=0))
    pooled = jnp.concatenate(pieces, axis=1)
    pooled_ref[...] = pooled
    wide = pooled.astype(jnp.float32)
    wide = wide - jnp.mean(wide, axis=-1, keepdims=True)
    spread = jnp.mean(wide * wide, axis=-1, keepdims=True)
    normed[...] = (wide * lax.rsqrt(spread + epsilon) * norm_ref[0:1] + norm_ref[1:2]).astype(
        jnp.bfloat16
    )
    nt = (((1,), (1,)), ((), ()))
    for k in range(4):
        rows = pl.ds(pl.multiple_of(lax.rem(x_at + y_lo + 4 - k, 4) * 448, 64), 448)
        proj[rows] = lax.dot_general(
            weights[2 * k][...], normed[:, pl.ds(near, 384)], nt,
            preferred_element_type=jnp.float32,
        ) + lax.dot_general(
            weights[2 * k + 1][...], normed[:, pl.ds(far, 384)], nt,
            preferred_element_type=jnp.float32,
        )
    for h in range(HEADS):
        q = (proj[h * KEY : (h + 1) * KEY] * KEY ** (-0.5)).astype(jnp.bfloat16)
        k = proj[512 + h * KEY : 512 + (h + 1) * KEY].astype(jnp.bfloat16)
        v = proj[1024 + h * VAL : 1024 + (h + 1) * VAL].astype(jnp.bfloat16)
        for d in (h, h + HEADS):
            out_ref[d, :KEY] = q
            out_ref[d, KEY : 2 * KEY] = k
            out_ref[d, 2 * KEY :] = v


def project(where, part, norm, weights):
    vmem = pl.BlockSpec(memory_space=pltpu.VMEM)
    return pl.pallas_call(
        project_kernel,
        out_shape=(
            jax.ShapeDtypeStruct((128, 768), jnp.bfloat16),
            jax.ShapeDtypeStruct((16, ROWS, 128), jnp.bfloat16),
        ),
        in_specs=[pl.BlockSpec(memory_space=pltpu.SMEM)] + [vmem] * 10,
        out_specs=(vmem, vmem),
        scratch_shapes=[
            pltpu.VMEM((128, 768), jnp.bfloat16),
            pltpu.VMEM((1792, 128), jnp.float32),
        ],
        compiler_params=pltpu.CompilerParams(vmem_limit_bytes=14 << 20),
        name="project",
    )(where, part, norm, *weights)


def on_device(
    sequence_input, bn_gain, bn_bias, conv_weight, conv_bias, ln_gain, ln_bias, qkv_weight
):
    raw = sequence_input[0]
    channels = raw.shape[1]
    y_lo = lax.axis_index("batch") // Z
    seq = lax.axis_index("seq")
    core, x_at = seq % 2, seq // 2 % 4
    where = jnp.stack([core, x_at, seq // 8, y_lo]).astype(jnp.int32)
    swap = [(i, i ^ 1) for i in range(16)]

    conv_half = lax.dynamic_slice(conv_weight.transpose(0, 2, 1), (0, 0, core * 384), (5, 24, 384))
    qkv_half = lax.dynamic_slice(qkv_weight.T, (0, core * 384), (56, 384))
    mine = jnp.concatenate(
        [
            conv_half.transpose(1, 0, 2).reshape(24, 1920),
            qkv_half.reshape(7, 8, 3, 128).transpose(2, 1, 0, 3).reshape(24, 896),
        ],
        axis=1,
    )
    mine = lax.ppermute(mine, ("batch", "seq"), quarters())

    pad = jnp.zeros((14, channels), raw.dtype)
    left = lax.ppermute(raw[-2:], "seq", [(i, i + 1) for i in range(15)])
    right = lax.ppermute(raw[:2], "seq", [(i + 1, i) for i in range(15)])
    block = jnp.concatenate([pad, left, raw, right, pad], axis=0)

    wide = raw.astype(jnp.float32)
    sums = jnp.stack([jnp.sum(wide, axis=0), jnp.sum(wide * wide, axis=0)])
    sums = jnp.sum(to_all(sums, "seq"), axis=0)
    sums, mine, block = lax.optimization_barrier((sums, mine, block))
    mine = to_all(mine, "batch", Z_GROUPS)
    blocks = [block] + [lax.ppermute(block, "seq", x_shift(k)) for k in range(1, 4)]
    sums, mine, blocks = lax.optimization_barrier((sums, mine, blocks))
    other = lax.ppermute(mine, "seq", swap)
    own = qkv_rows(mine)
    right, left = (lax.ppermute(own, "seq", x_shift(k)) for k in (1, 3))
    sums = jnp.sum(to_all(sums, "batch"), axis=0)
    sums, right, left = lax.optimization_barrier((sums, right, left))
    near = [right, lax.ppermute(right, "seq", x_shift(1)), left]
    count = float(raw.shape[0] * lax.axis_size("batch") * lax.axis_size("seq"))

    part = conv_block(
        where, blocks, sums, jnp.stack([bn_gain, bn_bias]), mine.reshape(192, 2816), other.reshape(192, 2816),
        lax.dynamic_slice(conv_bias, ((y_lo + x_at) % 4 * 192,), (192,))[None], count,
    )
    near, other = lax.optimization_barrier((part, near, other))[1:]
    weights = [own, qkv_rows(other)]
    for values in near:
        weights += [values, lax.ppermute(values, "seq", swap)]
    part = lax.all_to_all(part, "seq", 0, 0, axis_index_groups=X_GROUPS, tiled=True)
    pooled, packed = project(where, part, jnp.stack([ln_gain, ln_bias]), weights)
    packed = lax.all_to_all(packed, "seq", 0, 0, tiled=True)
    out = attend((seq // 8 * 8).astype(jnp.int32)[None], packed)
    out = lax.all_to_all(out, "seq", 0, 0, axis_index_groups=HALF_GROUPS, tiled=True)
    attended = out.reshape(HEADS * VAL, 128).T
    return (pooled[None], attended[None])


def solution(mesh):
    placed = (
        P("batch", "seq", None),
        P(),
        P(),
        P(None, None, "batch"),
        P(),
        P(),
        P(),
        P(None, "batch"),
    )
    return jax.shard_map(
        on_device,
        mesh=mesh,
        in_specs=placed,
        out_specs=(P("batch", "seq", None), P("batch", "seq", None)),
        check_vma=False,
    )
```

time: 204 us -> 182 us (0.89)
  the two profiles are of different devices: /device:TPU:8 before, /device:TPU:16 now
where the time goes in v2:
time: 182 us; the launch traced here: 181 us
  starting transfers between devices  73 us (40%)
  waiting for transfers between devices  65.9 us (36%)
  Pallas kernels  17.7 us (10%)
  local copies, waits for them, and re-layouts  11.7 us (6%)
  blocking collectives  9.58 us (5%)
  other arithmetic  2.29 us (1%)
    all_to_all x3, starting transfers between devices, to_all(): lax.all_to_all(jnp.broadcast_to(values[None], (count,) + values.shape), a...  30.9 us
    all_to_all x1, waiting for transfers between devices, on_device(): packed = lax.all_to_all(packed, 'seq', 0, 0, tiled=True)  28.8 us
    ppermute x3, waiting for transfers between devices, on_device(): lax.ppermute(block, 'seq', x_shift(k))  13.3 us
    all_to_all x3, waiting for transfers between devices, to_all(): lax.all_to_all(jnp.broadcast_to(values[None], (count,) + values.shape), a...  11 us
    all_to_all x1, blocking collectives, on_device(): lax.all_to_all(out, 'seq', 0, 0, axis_index_groups=HALF_GROUPS, tiled=True)  9.58 us
    ppermute x3, starting transfers between devices, on_device(): lax.ppermute(block, 'seq', x_shift(k))  9.51 us
    pallas_call x1, Pallas kernels, conv_block(): pl.pallas_call(functools.partial(conv_kernel, count=count), out_shape=jax...  9.51 us
    ppermute x2, starting transfers between devices, on_device(): right, left = (lax.ppermute(own, 'seq', x_shift(k)) for k in (1, 3))  7.05 us
  transfers between devices with their start and end apart: 18, of which 11 were waited for; matrix products, arithmetic and copies ran while one was open for 3% of the time, Pallas kernels for 5%

profile of v2, /device:TPU:16, one launch (start us, length us, event | category | flops | bytes accessed | tf_op | source)
XLA Modules:
  0.0 181.3 jit_solution(11596961998097766431)
XLA Ops:
  4.9 11.2 %all-to-all-start = ((f32[16,2,768]{2,1,0:T(2,128)}), f32[16,2,768]{2,1,0:T(2,128)S(1)}, u32[]{:S(2)}, u32[]{:S(2)}) async-start(f32[16,2,768]{2,1,0:T(2,128)} %broadcast_in_dim.16), calls=%async_computation | async-start | bytes 196608 | tf_op jit(solution)/shard_map/all_to_all | solution.py:40
  16.2 2.3 %collective-permute-start.1 = (bf16[2,768]{1,0:T(2,128)(2,1)S(1)}, bf16[2,768]{1,0:T(2,128)(2,1)S(1)}, u32[]{:S(2)}, u32[]{:S(2)}) collective-permute-start(bf16[2,768]{1,0:T(2,128)(2,1)S(1)} %get-tuple-element.41), channel_id=1, source_target_pairs={{0,1},{1,2},{2,3},{3,4},{4,5},{5,6},{6,7},{7,8},{8,9},{9,10},{10,1... | collective-permute-start | bytes 9224 | tf_op jit(solution)/shard_map/ppermute | solution.py:241
  19.8 2.9 %collective-permute-done.2 = bf16[2,768]{1,0:T(2,128)(2,1)S(1)} collective-permute-done((bf16[2,768]{1,0:T(2,128)(2,1)S(1)}, bf16[2,768]{1,0:T(2,128)(2,1)S(1)}, u32[]{:S(2)}, u32[]{:S(2)}) %collective-permute-start.2) | collective-permute-done | bytes 3104 | tf_op jit(solution)/shard_map/ppermute | solution.py:242
  23.0 4.3 %all-to-all-done = f32[16,2,768]{2,1,0:T(2,128)S(1)} async-done(((f32[16,2,768]{2,1,0:T(2,128)}), f32[16,2,768]{2,1,0:T(2,128)S(1)}, u32[]{:S(2)}, u32[]{:S(2)}) %all-to-all-start) | async-done | bytes 98336 | tf_op jit(solution)/shard_map/all_to_all | solution.py:40
  28.4 10.3 %all-to-all-start.1 = ((bf16[8,24,2816]{2,1,0:T(8,128)(2,1)}), bf16[8,24,2816]{2,1,0:T(8,128)(2,1)S(1)}, u32[]{:S(2)}, u32[]{:S(2)}) async-start(bf16[8,24,2816]{2,1,0:T(8,128)(2,1)} %broadcast_in_dim.35), calls=%async_computation.1 | async-start | bytes 2162688 | tf_op jit(solution)/shard_map/all_to_all | solution.py:40
  38.7 2.3 %collective-permute-start.3 = (bf16[288,768]{1,0:T(8,128)(2,1)S(1)}, bf16[288,768]{1,0:T(8,128)(2,1)S(1)}, u32[]{:S(2)}, u32[]{:S(2)}) collective-permute-start(bf16[288,768]{1,0:T(8,128)(2,1)S(1)} %concatenate.7.x0), channel_id=1, source_target_pairs={{0,2},{1,3},{2,4},{3,5},{4,6},{5,7},{6,0},{7,1},{8,10},{9,11},{10,... | collective-permute-start | bytes 1327112 | tf_op jit(solution)/shard_map/ppermute | solution.py:250
  41.0 5.3 %collective-permute-start.4 = (bf16[288,768]{1,0:T(8,128)(2,1)S(1)}, bf16[288,768]{1,0:T(8,128)(2,1)S(1)}, u32[]{:S(2)}, u32[]{:S(2)}) collective-permute-start(bf16[288,768]{1,0:T(8,128)(2,1)S(1)} %concatenate.7.x0), channel_id=1, source_target_pairs={{0,4},{1,5},{2,6},{3,7},{4,0},{5,1},{6,2},{7,3},{8,12},{9,13},{10,... | collective-permute-start | bytes 1327112 | tf_op jit(solution)/shard_map/ppermute | solution.py:250
  51.2 6.5 %collective-permute-done.4.x2 = bf16[288,768]{1,0:T(8,128)(2,1)S(1)} collective-permute-done((bf16[288,768]{1,0:T(8,128)(2,1)S(1)}, bf16[288,768]{1,0:T(8,128)(2,1)S(1)}, u32[]{:S(2)}, u32[]{:S(2)}) %collective-permute-start.4) | collective-permute-done | bytes 442400 | tf_op jit(solution)/shard_map/ppermute | solution.py:250
  58.5 4.6 %collective-permute-done.5.x3 = bf16[288,768]{1,0:T(8,128)(2,1)S(1)} collective-permute-done((bf16[288,768]{1,0:T(8,128)(2,1)S(1)}, bf16[288,768]{1,0:T(8,128)(2,1)S(1)}, u32[]{:S(2)}, u32[]{:S(2)}) %collective-permute-start.5) | collective-permute-done | bytes 442400 | tf_op jit(solution)/shard_map/ppermute | solution.py:250
  63.9 4.5 %all-to-all-done.1 = bf16[8,24,2816]{2,1,0:T(8,128)(2,1)S(1)} async-done(((bf16[8,24,2816]{2,1,0:T(8,128)(2,1)}), bf16[8,24,2816]{2,1,0:T(8,128)(2,1)S(1)}, u32[]{:S(2)}, u32[]{:S(2)}) %all-to-all-start.1) | async-done | bytes 1081376 | tf_op jit(solution)/shard_map/all_to_all | solution.py:40
  71.1 9.3 %all-to-all-start.2 = ((f32[32,2,768]{2,1,0:T(2,128)}), f32[32,2,768]{2,1,0:T(2,128)}, u32[]{:S(2)}, u32[]{:S(2)}) async-start(f32[32,2,768]{2,1,0:T(2,128)} %broadcast_in_dim.36), calls=%async_computation.2 | async-start | bytes 393216 | tf_op jit(solution)/shard_map/all_to_all | solution.py:40
  80.5 2.3 %collective-permute-start.6 = (bf16[448,384]{1,0:T(8,128)(2,1)S(1)}, bf16[448,384]{1,0:T(8,128)(2,1)S(1)}, u32[]{:S(2)}, u32[]{:S(2)}) collective-permute-start(bf16[448,384]{1,0:T(8,128)(2,1)S(1)} %bitcast.45), channel_id=1, source_target_pairs={{0,2},{1,3},{2,4},{3,5},{4,6},{5,7},{6,0},{7,1},{8,10},{9,11},{10,... | collective-permute-start | bytes 1032200 | tf_op jit(solution)/shard_map/ppermute | solution.py:254
  82.8 4.7 %collective-permute-start.7 = (bf16[448,384]{1,0:T(8,128)(2,1)S(1)}, bf16[448,384]{1,0:T(8,128)(2,1)}, u32[]{:S(2)}, u32[]{:S(2)}) collective-permute-start(bf16[448,384]{1,0:T(8,128)(2,1)S(1)} %bitcast.46), channel_id=1, source_target_pairs={{0,6},{1,7},{2,0},{3,1},{4,2},{5,3},{6,4},{7,5},{8,14},{9,15},{10,... | collective-permute-start | bytes 1032200 | tf_op jit(solution)/shard_map/ppermute | solution.py:254
  87.5 2.3 %all-to-all-done.2 = f32[32,2,768]{2,1,0:T(2,128)} async-done(((f32[32,2,768]{2,1,0:T(2,128)}), f32[32,2,768]{2,1,0:T(2,128)}, u32[]{:S(2)}, u32[]{:S(2)}) %all-to-all-start.2) | async-done | bytes 196640 | tf_op jit(solution)/shard_map/all_to_all | solution.py:40
  94.2 3.5 %collective-permute-start.9 = (bf16[448,384]{1,0:T(8,128)(2,1)S(1)}, bf16[448,384]{1,0:T(8,128)(2,1)}, u32[]{:S(2)}, u32[]{:S(2)}) collective-permute-start(bf16[448,384]{1,0:T(8,128)(2,1)S(1)} %collective-permute-done.6.refs_2_), channel_id=1, source_target_pairs={{0,2},{1,3},{2,4},{3,5},{4,6},{5,7},{6,0},{7,1},{8,10},{9,11},{10,... | collective-permute-start | bytes 1032200 | tf_op jit(solution)/shard_map/ppermute | solution.py:257
  101.8 9.5 %conv_block.1 = bf16[4,192,128]{2,1,0:T(8,128)(2,1)} custom-call(s32[4]{0:T(128)S(1)} %pad_add_fusion.where_ref, bf16[288,768]{1,0:T(8,128)(2,1)S(1)} %concatenate.7.x0, bf16[288,768]{1,0:T(8,128)(2,1)S(1)} %copy-done.2, bf16[288,768]{1,0:T(8,128)(2,1)S(1)} %copy-done.4, bf16[288,768]{1,0:T(8,128)(2,1)S(1)} %copy-done.6, f32[2,768]{1,0:T(2,128)S(1)} %reduce_sum.39.sums_ref, ...), custom_call_target="tpu_custom_call" | custom-call | tf_op jit(solution)/shard_map/conv_block/pallas_call | solution.py:143
  113.2 2.4 %collective-permute-start.11 = (bf16[448,384]{1,0:T(8,128)(2,1)}, bf16[448,384]{1,0:T(8,128)(2,1)S(1)}, u32[]{:S(2)}, u32[]{:S(2)}) collective-permute-start(bf16[448,384]{1,0:T(8,128)(2,1)} %collective-permute-done.9.refs_4_), channel_id=1, source_target_pairs={{0,1},{1,0},{2,3},{3,2},{4,5},{5,4},{6,7},{7,6},{8,9},{9,8},{10,11... | collective-permute-start | bytes 1032200 | tf_op jit(solution)/shard_map/ppermute | solution.py:267
  117.6 4.9 %all-to-all-start.3 = ((bf16[4,192,128]{2,1,0:T(8,128)(2,1)}), bf16[4,192,128]{2,1,0:T(8,128)(2,1)S(1)}, u32[]{:S(2)}, u32[]{:S(2)}) async-start(bf16[4,192,128]{2,1,0:T(8,128)(2,1)} %conv_block.1), calls=%async_computation.3 | async-start | bytes 393216 | tf_op jit(solution)/shard_map/all_to_all | solution.py:268
  122.6 6.5 %all-to-all-done.3.part_ref = bf16[4,192,128]{2,1,0:T(8,128)(2,1)S(1)} async-done(((bf16[4,192,128]{2,1,0:T(8,128)(2,1)}), bf16[4,192,128]{2,1,0:T(8,128)(2,1)S(1)}, u32[]{:S(2)}, u32[]{:S(2)}) %all-to-all-start.3) | async-done | bytes 196640 | tf_op jit(solution)/shard_map/all_to_all | solution.py:268
  129.2 3.5 %project.1 = (bf16[128,768]{1,0:T(8,128)(2,1)}, bf16[16,224,128]{2,1,0:T(8,128)(2,1)}) custom-call(s32[4]{0:T(128)S(1)} %pad_add_fusion.where_ref, bf16[4,192,128]{2,1,0:T(8,128)(2,1)S(1)} %all-to-all-done.3.part_ref, f32[2,768]{1,0:T(2,128)S(1)} %pad_maximum_fusion.3.norm_ref, bf16[448,384]{1,0:T(8,128)(2,1)S(1)} %bitcast.47, ...), custom_call_target="tpu_custom_call" | custom-call | tf_op jit(solution)/shard_map/project/pallas_call | solution.py:201
  132.7 4.7 %all-to-all-start.4 = ((bf16[16,224,128]{2,1,0:T(8,128)(2,1)}), bf16[16,224,128]{2,1,0:T(8,128)(2,1)S(1)}, u32[]{:S(2)}, u32[]{:S(2)}) async-start(bf16[16,224,128]{2,1,0:T(8,128)(2,1)} %get-tuple-element.37), calls=%async_computation.4 | async-start | bytes 1835008 | tf_op jit(solution)/shard_map/all_to_all | solution.py:270
  137.4 28.8 %all-to-all-done.4.r_ref = bf16[16,224,128]{2,1,0:T(8,128)(2,1)S(1)} async-done(((bf16[16,224,128]{2,1,0:T(8,128)(2,1)}), bf16[16,224,128]{2,1,0:T(8,128)(2,1)S(1)}, u32[]{:S(2)}, u32[]{:S(2)}) %all-to-all-start.4) | async-done | bytes 917536 | tf_op jit(solution)/shard_map/all_to_all | solution.py:270
  166.2 4.7 %attend.1 = bf16[8,96,128]{2,1,0:T(8,128)(2,1)S(1)} custom-call(s32[1]{0:T(128)} %bitcast.22.first_ref, bf16[16,224,128]{2,1,0:T(8,128)(2,1)S(1)} %all-to-all-done.4.r_ref), custom_call_target="tpu_custom_call" | custom-call | tf_op jit(solution)/shard_map/attend/pallas_call | solution.py:67
  170.9 9.6 %all_to_all.30 = bf16[8,96,128]{2,1,0:T(8,128)(2,1)S(1)} all-to-all(bf16[8,96,128]{2,1,0:T(8,128)(2,1)S(1)} %attend.1), channel_id=1, replica_groups={{0,1,2,3,4,5,6,7},{8,9,10,11,12,13,14,15},{16,17,18,19,20,21,22,23},{24..., dimensions={0} | all-to-all | bytes 393216 | tf_op jit(solution)/shard_map/all_to_all | solution.py:272
  (69 shorter events, 29.1 us)
Async XLA Ops:
  0.6 15.5 %copy-start.7 = (bf16[1,256,768]{2,1,0:T(8,128)(2,1)S(1)}, bf16[1,256,768]{2,1,0:T(8,128)(2,1)}, u32[]{:S(2)}) copy-start(bf16[1,256,768]{2,1,0:T(8,128)(2,1)} %param.8) | copy-start | bytes 1179652
  2.4 24.9 %collective-permute-start = (bf16[24,2816]{1,0:T(8,128)(2,1)S(1)}, bf16[24,2816]{1,0:T(8,128)(2,1)S(1)}, u32[]{:S(2)}, u32[]{:S(2)}) collective-permute-start(bf16[24,2816]{1,0:T(8,128)(2,1)S(1)} %pad_maximum_fusion), channel_id=1, source_target_pairs={{0,0},{1,1},{130,2},{131,3},{260,4},{261,5},{398,6},{399,7},{8,8},... | collective-permute-start | bytes 405512 | tf_op jit(solution)/shard_map/ppermute | solution.py:238
  4.9 22.4 %all-to-all-start = ((f32[16,2,768]{2,1,0:T(2,128)}), f32[16,2,768]{2,1,0:T(2,128)S(1)}, u32[]{:S(2)}, u32[]{:S(2)}) async-start(f32[16,2,768]{2,1,0:T(2,128)} %broadcast_in_dim.16), calls=%async_computation | async-start | bytes 196608 | tf_op jit(solution)/shard_map/all_to_all | solution.py:40
  16.2 3.6 %collective-permute-start.1 = (bf16[2,768]{1,0:T(2,128)(2,1)S(1)}, bf16[2,768]{1,0:T(2,128)(2,1)S(1)}, u32[]{:S(2)}, u32[]{:S(2)}) collective-permute-start(bf16[2,768]{1,0:T(2,128)(2,1)S(1)} %get-tuple-element.41), channel_id=1, source_target_pairs={{0,1},{1,2},{2,3},{3,4},{4,5},{5,6},{6,7},{7,8},{8,9},{9,10},{10,1... | collective-permute-start | bytes 9224 | tf_op jit(solution)/shard_map/ppermute | solution.py:241
  18.5 4.2 %collective-permute-start.2 = (bf16[2,768]{1,0:T(2,128)(2,1)S(1)}, bf16[2,768]{1,0:T(2,128)(2,1)S(1)}, u32[]{:S(2)}, u32[]{:S(2)}) collective-permute-start(bf16[2,768]{1,0:T(2,128)(2,1)S(1)} %get-tuple-element.40), channel_id=1, source_target_pairs={{1,0},{2,1},{3,2},{4,3},{5,4},{6,5},{7,6},{8,7},{9,8},{10,9},{11,1... | collective-permute-start | bytes 9224 | tf_op jit(solution)/shard_map/ppermute | solution.py:242
  28.4 40.0 %all-to-all-start.1 = ((bf16[8,24,2816]{2,1,0:T(8,128)(2,1)}), bf16[8,24,2816]{2,1,0:T(8,128)(2,1)S(1)}, u32[]{:S(2)}, u32[]{:S(2)}) async-start(bf16[8,24,2816]{2,1,0:T(8,128)(2,1)} %broadcast_in_dim.35), calls=%async_computation.1 | async-start | bytes 2162688 | tf_op jit(solution)/shard_map/all_to_all | solution.py:40
  38.7 11.7 %collective-permute-start.3 = (bf16[288,768]{1,0:T(8,128)(2,1)S(1)}, bf16[288,768]{1,0:T(8,128)(2,1)S(1)}, u32[]{:S(2)}, u32[]{:S(2)}) collective-permute-start(bf16[288,768]{1,0:T(8,128)(2,1)S(1)} %concatenate.7.x0), channel_id=1, source_target_pairs={{0,2},{1,3},{2,4},{3,5},{4,6},{5,7},{6,0},{7,1},{8,10},{9,11},{10,... | collective-permute-start | bytes 1327112 | tf_op jit(solution)/shard_map/ppermute | solution.py:250
  41.0 16.7 %collective-permute-start.4 = (bf16[288,768]{1,0:T(8,128)(2,1)S(1)}, bf16[288,768]{1,0:T(8,128)(2,1)S(1)}, u32[]{:S(2)}, u32[]{:S(2)}) collective-permute-start(bf16[288,768]{1,0:T(8,128)(2,1)S(1)} %concatenate.7.x0), channel_id=1, source_target_pairs={{0,4},{1,5},{2,6},{3,7},{4,0},{5,1},{6,2},{7,3},{8,12},{9,13},{10,... | collective-permute-start | bytes 1327112 | tf_op jit(solution)/shard_map/ppermute | solution.py:250
  46.3 16.8 %collective-permute-start.5 = (bf16[288,768]{1,0:T(8,128)(2,1)S(1)}, bf16[288,768]{1,0:T(8,128)(2,1)S(1)}, u32[]{:S(2)}, u32[]{:S(2)}) collective-permute-start(bf16[288,768]{1,0:T(8,128)(2,1)S(1)} %concatenate.7.x0), channel_id=1, source_target_pairs={{0,6},{1,7},{2,0},{3,1},{4,2},{5,3},{6,4},{7,5},{8,14},{9,15},{10,... | collective-permute-start | bytes 1327112 | tf_op jit(solution)/shard_map/ppermute | solution.py:250
  68.4 30.3 %collective-permute-start.8 = (bf16[8,24,2816]{2,1,0:T(8,128)(2,1)S(1)}, bf16[8,24,2816]{2,1,0:T(8,128)(2,1)S(1)}, u32[]{:S(2)}, u32[]{:S(2)}) collective-permute-start(bf16[8,24,2816]{2,1,0:T(8,128)(2,1)S(1)} %all-to-all-done.1), channel_id=1, source_target_pairs={{0,1},{1,0},{2,3},{3,2},{4,5},{5,4},{6,7},{7,6},{8,9},{9,8},{10,11... | collective-permute-start | bytes 3244040 | tf_op jit(solution)/shard_map/ppermute | solution.py:252
  71.0 26.7 %copy-start.8 = (f32[768]{0:T(1024)S(1)}, f32[768]{0:T(1024)}, u32[]{:S(2)}) copy-start(f32[768]{0:T(1024)} %param.9) | copy-start | bytes 9220
  71.0 26.8 %copy-start.9 = (f32[768]{0:T(1024)S(1)}, f32[768]{0:T(1024)}, u32[]{:S(2)}) copy-start(f32[768]{0:T(1024)} %param.10) | copy-start | bytes 9220
  71.0 26.8 %copy-start.10 = (f32[768]{0:T(1024)S(1)}, f32[768]{0:T(1024)}, u32[]{:S(2)}) copy-start(f32[768]{0:T(1024)} %param.13) | copy-start | bytes 9220
  71.0 26.8 %copy-start.11 = (f32[768]{0:T(1024)S(1)}, f32[768]{0:T(1024)}, u32[]{:S(2)}) copy-start(f32[768]{0:T(1024)} %param.14) | copy-start | bytes 9220
  71.1 18.8 %all-to-all-start.2 = ((f32[32,2,768]{2,1,0:T(2,128)}), f32[32,2,768]{2,1,0:T(2,128)}, u32[]{:S(2)}, u32[]{:S(2)}) async-start(f32[32,2,768]{2,1,0:T(2,128)} %broadcast_in_dim.36), calls=%async_computation.2 | async-start | bytes 393216 | tf_op jit(solution)/shard_map/all_to_all | solution.py:40
  80.5 12.5 %collective-permute-start.6 = (bf16[448,384]{1,0:T(8,128)(2,1)S(1)}, bf16[448,384]{1,0:T(8,128)(2,1)S(1)}, u32[]{:S(2)}, u32[]{:S(2)}) collective-permute-start(bf16[448,384]{1,0:T(8,128)(2,1)S(1)} %bitcast.45), channel_id=1, source_target_pairs={{0,2},{1,3},{2,4},{3,5},{4,6},{5,7},{6,0},{7,1},{8,10},{9,11},{10,... | collective-permute-start | bytes 1032200 | tf_op jit(solution)/shard_map/ppermute | solution.py:254
  82.8 11.4 %collective-permute-start.7 = (bf16[448,384]{1,0:T(8,128)(2,1)S(1)}, bf16[448,384]{1,0:T(8,128)(2,1)}, u32[]{:S(2)}, u32[]{:S(2)}) collective-permute-start(bf16[448,384]{1,0:T(8,128)(2,1)S(1)} %bitcast.46), channel_id=1, source_target_pairs={{0,6},{1,7},{2,0},{3,1},{4,2},{5,3},{6,4},{7,5},{8,14},{9,15},{10,... | collective-permute-start | bytes 1032200 | tf_op jit(solution)/shard_map/ppermute | solution.py:254
  94.2 17.1 %collective-permute-start.9 = (bf16[448,384]{1,0:T(8,128)(2,1)S(1)}, bf16[448,384]{1,0:T(8,128)(2,1)}, u32[]{:S(2)}, u32[]{:S(2)}) collective-permute-start(bf16[448,384]{1,0:T(8,128)(2,1)S(1)} %collective-permute-done.6.refs_2_), channel_id=1, source_target_pairs={{0,2},{1,3},{2,4},{3,5},{4,6},{5,7},{6,0},{7,1},{8,10},{9,11},{10,... | collective-permute-start | bytes 1032200 | tf_op jit(solution)/shard_map/ppermute | solution.py:257
  98.7 1.0 copy-start.2
  111.3 17.8 %collective-permute-start.10 = (bf16[448,384]{1,0:T(8,128)(2,1)S(1)}, bf16[448,384]{1,0:T(8,128)(2,1)S(1)}, u32[]{:S(2)}, u32[]{:S(2)}) collective-permute-start(bf16[448,384]{1,0:T(8,128)(2,1)S(1)} %collective-permute-done.6.refs_2_), channel_id=1, source_target_pairs={{0,1},{1,0},{2,3},{3,2},{4,5},{5,4},{6,7},{7,6},{8,9},{9,8},{10,11... | collective-permute-start | bytes 1032200 | tf_op jit(solution)/shard_map/ppermute | solution.py:267
  113.2 15.9 %collective-permute-start.11 = (bf16[448,384]{1,0:T(8,128)(2,1)}, bf16[448,384]{1,0:T(8,128)(2,1)S(1)}, u32[]{:S(2)}, u32[]{:S(2)}) collective-permute-start(bf16[448,384]{1,0:T(8,128)(2,1)} %collective-permute-done.9.refs_4_), channel_id=1, source_target_pairs={{0,1},{1,0},{2,3},{3,2},{4,5},{5,4},{6,7},{7,6},{8,9},{9,8},{10,11... | collective-permute-start | bytes 1032200 | tf_op jit(solution)/shard_map/ppermute | solution.py:267
  115.7 13.5 %collective-permute-start.12 = (bf16[448,384]{1,0:T(8,128)(2,1)}, bf16[448,384]{1,0:T(8,128)(2,1)}, u32[]{:S(2)}, u32[]{:S(2)}) collective-permute-start(bf16[448,384]{1,0:T(8,128)(2,1)} %collective-permute-done.7.refs_6_), channel_id=1, source_target_pairs={{0,1},{1,0},{2,3},{3,2},{4,5},{5,4},{6,7},{7,6},{8,9},{9,8},{10,11... | collective-permute-start | bytes 1032200 | tf_op jit(solution)/shard_map/ppermute | solution.py:267
  117.6 11.5 %all-to-all-start.3 = ((bf16[4,192,128]{2,1,0:T(8,128)(2,1)}), bf16[4,192,128]{2,1,0:T(8,128)(2,1)S(1)}, u32[]{:S(2)}, u32[]{:S(2)}) async-start(bf16[4,192,128]{2,1,0:T(8,128)(2,1)} %conv_block.1), calls=%async_computation.3 | async-start | bytes 393216 | tf_op jit(solution)/shard_map/all_to_all | solution.py:268
  132.7 33.5 %all-to-all-start.4 = ((bf16[16,224,128]{2,1,0:T(8,128)(2,1)}), bf16[16,224,128]{2,1,0:T(8,128)(2,1)S(1)}, u32[]{:S(2)}, u32[]{:S(2)}) async-start(bf16[16,224,128]{2,1,0:T(8,128)(2,1)} %get-tuple-element.37), calls=%async_computation.4 | async-start | bytes 1835008 | tf_op jit(solution)/shard_map/all_to_all | solution.py:270
  (6 other events, 5.3 us)

commit v3 on v2

--- a/solution.py
+++ b/solution.py
@@ -78,8 +78,9 @@
 
 
 def conv_kernel(where_ref, x0, x1, x2, x3, sums_ref, norm_ref, mine_ref, other_ref, bias_ref,
-                out_ref, act, product, held, arrived, *, count):
+                out_ref, act, product, *, count):
     core, x_at, y_hi = where_ref[0], where_ref[1], where_ref[2]
+    bias = bias_ref[pl.ds(lax.rem(x_at + where_ref[3], 4), 1)]
     mean = sums_ref[0:1] / count
     scale = lax.rsqrt(sums_ref[1:2] / count - mean * mean + epsilon) * norm_ref[0:1]
     shift = norm_ref[1:2]
@@ -91,26 +92,19 @@
             (values.astype(jnp.float32) - mean) * scale + shift, approximate=True
         ).astype(jnp.bfloat16)
 
-    copies = [
-        pltpu.make_async_copy(x_ref, held.at[k], arrived.at[k])
-        for k, x_ref in enumerate((x0, x1, x2, x3))
-    ]
-    for copy in copies:
-        copy.start()
-    for k in range(4):
-        copies[k].wait()
+    for k, x_ref in enumerate((x0, x1, x2, x3)):
         slot = lax.rem(x_at + 4 - k, 4)
         seq = y_hi * 8 + slot * 2 + core
-        edge = activated(held[k, 0:16])
+        edge = activated(x_ref[0:16])
         row = lax.broadcasted_iota(jnp.int32, edge.shape, 0)
         act[k, 0:16] = jnp.where((row >= 14) & (seq > 0), edge, jnp.zeros_like(edge))
-        edge = activated(held[k, 272:288])
+        edge = activated(x_ref[272:288])
         act[k, 272:288] = jnp.where((row < 2) & (seq < 15), edge, jnp.zeros_like(edge))
 
         @pl.loop(1, 17)
         def _(i):
             rows = pl.ds(pl.multiple_of(i * 16, 16), 16)
-            act[k, rows] = activated(held[k, rows])
+            act[k, rows] = activated(x_ref[rows])
 
         for tap in range(5):
             nt = (((1,), (1,)), ((), ()))
@@ -129,7 +123,7 @@
                     total = total + product[base + tap, pl.ds(14 + odd + tap, 128, stride=2), :]
                 pair.append(total[:, :lanes])
             columns = slice(base // 5 * 128, base // 5 * 128 + lanes)
-            pooled = jnp.maximum(pair[0], pair[1]) + bias_ref[:, columns]
+            pooled = jnp.maximum(pair[0], pair[1]) + bias[:, columns]
             pooled = pooled.astype(jnp.bfloat16)
             if base == 0:
                 out_ref[slot, :128] = pooled
@@ -143,15 +137,11 @@
     return pl.pallas_call(
         functools.partial(conv_kernel, count=count),
         out_shape=jax.ShapeDtypeStruct((4, 192, 128), jnp.bfloat16),
-        in_specs=[pl.BlockSpec(memory_space=pltpu.SMEM)]
-        + [pl.BlockSpec(memory_space=pl.ANY)] * 4
-        + [vmem] * 5,
+        in_specs=[pl.BlockSpec(memory_space=pltpu.SMEM)] + [vmem] * 9,
         out_specs=vmem,
         scratch_shapes=[
             pltpu.VMEM((4, 288, 768), jnp.bfloat16),
             pltpu.VMEM((10, 288, 128), jnp.float32),
-            pltpu.VMEM((4, 288, 768), jnp.bfloat16),
-            pltpu.SemaphoreType.DMA((4,)),
         ],
         compiler_params=pltpu.CompilerParams(vmem_limit_bytes=14 << 20),
         name="conv_block",
@@ -159,7 +149,7 @@
 
 
 def project_kernel(where_ref, part_ref, norm_ref, *refs):
-    weights, (pooled_ref, out_ref, normed, proj) = refs[:8], refs[8:]
+    weights, (pooled_ref, out_ref, normed, proj) = refs[:6], refs[6:]
     core, x_at, y_lo = where_ref[0], where_ref[1], where_ref[3]
     near = pl.multiple_of(core * 384, 128)
     far = pl.multiple_of(384 - core * 384, 128)
@@ -180,10 +170,10 @@
     for k in range(4):
         rows = pl.ds(pl.multiple_of(lax.rem(x_at + y_lo + 4 - k, 4) * 448, 64), 448)
         proj[rows] = lax.dot_general(
-            weights[2 * k][...], normed[:, pl.ds(near, 384)], nt,
+            weights[k][...], normed[:, pl.ds(near, 384)], nt,
             preferred_element_type=jnp.float32,
         ) + lax.dot_general(
-            weights[2 * k + 1][...], normed[:, pl.ds(far, 384)], nt,
+            weights[4][...] if k == 0 else weights[5][(k - 1) * 448 : k * 448], normed[:, pl.ds(far, 384)], nt,
             preferred_element_type=jnp.float32,
         )
     for h in range(HEADS):
@@ -204,7 +194,7 @@
             jax.ShapeDtypeStruct((128, 768), jnp.bfloat16),
             jax.ShapeDtypeStruct((16, ROWS, 128), jnp.bfloat16),
         ),
-        in_specs=[pl.BlockSpec(memory_space=pltpu.SMEM)] + [vmem] * 10,
+        in_specs=[pl.BlockSpec(memory_space=pltpu.SMEM)] + [vmem] * 8,
         out_specs=(vmem, vmem),
         scratch_shapes=[
             pltpu.VMEM((128, 768), jnp.bfloat16),
@@ -244,27 +234,26 @@
 
     wide = raw.astype(jnp.float32)
     sums = jnp.stack([jnp.sum(wide, axis=0), jnp.sum(wide * wide, axis=0)])
-    sums = jnp.sum(to_all(sums, "seq"), axis=0)
     sums, mine, block = lax.optimization_barrier((sums, mine, block))
     mine = to_all(mine, "batch", Z_GROUPS)
+    for bit in (1, 2, 4, 8):
+        sums = sums + lax.ppermute(sums, "seq", [(i, i ^ bit) for i in range(16)])
+    sums, block = lax.optimization_barrier((sums, block))
     blocks = [block] + [lax.ppermute(block, "seq", x_shift(k)) for k in range(1, 4)]
-    sums, mine, blocks = lax.optimization_barrier((sums, mine, blocks))
+    sums, mine = lax.optimization_barrier((sums, mine))
     other = lax.ppermute(mine, "seq", swap)
     own = qkv_rows(mine)
-    right, left = (lax.ppermute(own, "seq", x_shift(k)) for k in (1, 3))
+    near = [lax.ppermute(own, "seq", x_shift(k)) for k in range(1, 4)]
     sums = jnp.sum(to_all(sums, "batch"), axis=0)
-    sums, right, left = lax.optimization_barrier((sums, right, left))
-    near = [right, lax.ppermute(right, "seq", x_shift(1)), left]
     count = float(raw.shape[0] * lax.axis_size("batch") * lax.axis_size("seq"))
 
     part = conv_block(
         where, blocks, sums, jnp.stack([bn_gain, bn_bias]), mine.reshape(192, 2816), other.reshape(192, 2816),
-        lax.dynamic_slice(conv_bias, ((y_lo + x_at) % 4 * 192,), (192,))[None], count,
+        conv_bias.reshape(4, 192), count,
     )
     near, other = lax.optimization_barrier((part, near, other))[1:]
-    weights = [own, qkv_rows(other)]
-    for values in near:
-        weights += [values, lax.ppermute(values, "seq", swap)]
+    far = lax.ppermute(jnp.concatenate(near, axis=0), "seq", swap)
+    weights = [own] + near + [qkv_rows(other), far]
     part = lax.all_to_all(part, "seq", 0, 0, axis_index_groups=X_GROUPS, tiled=True)
     pooled, packed = project(where, part, jnp.stack([ln_gain, ln_bias]), weights)
     packed = lax.all_to_all(packed, "seq", 0, 0, tiled=True)

time: 182 us -> 170 us (0.934)
  the two profiles are of different devices: /device:TPU:16 before, /device:TPU:8 now
where the time goes in v3:
time: 170 us; the launch traced here: 169 us
  starting transfers between devices  81.2 us (48%)
  waiting for transfers between devices  50.4 us (30%)
  Pallas kernels  17.5 us (10%)
  blocking collectives  9.23 us (5%)
  local copies, waits for them, and re-layouts  4.92 us (3%)
  other arithmetic  4.42 us (3%)
    all_to_all x1, waiting for transfers between devices, on_device(): packed = lax.all_to_all(packed, 'seq', 0, 0, tiled=True)  28.8 us
    ppermute x4, starting transfers between devices, on_device(): sums = sums + lax.ppermute(sums, 'seq', [(i, i ^ bit) for i in range(16)])  23.7 us
    all_to_all x2, starting transfers between devices, to_all(): lax.all_to_all(jnp.broadcast_to(values[None], (count,) + values.shape), a...  19.6 us
    ppermute x3, starting transfers between devices, on_device(): lax.ppermute(block, 'seq', x_shift(k))  11.9 us
    ppermute x3, starting transfers between devices, on_device(): near = [lax.ppermute(own, 'seq', x_shift(k)) for k in range(1, 4)]  9.82 us
    ppermute x4, waiting for transfers between devices, on_device(): sums = sums + lax.ppermute(sums, 'seq', [(i, i ^ bit) for i in range(16)])  9.56 us
    all_to_all x1, blocking collectives, on_device(): lax.all_to_all(out, 'seq', 0, 0, axis_index_groups=HALF_GROUPS, tiled=True)  9.23 us
    pallas_call x1, Pallas kernels, conv_block(): pl.pallas_call(functools.partial(conv_kernel, count=count), out_shape=jax...  9.04 us
  transfers between devices with their start and end apart: 19, of which 9 were waited for; matrix products, arithmetic and copies ran while one was open for 3% of the time, Pallas kernels for 5%

profile of v3, /device:TPU:8, one launch (start us, length us, event | category | flops | bytes accessed | tf_op | source)
XLA Modules:
  0.0 168.8 jit_solution(4398445479728508335)
XLA Ops:
  7.2 3.6 %collective-permute-done.2 = bf16[2,768]{1,0:T(2,128)(2,1)S(1)} collective-permute-done((bf16[2,768]{1,0:T(2,128)(2,1)S(1)}, bf16[2,768]{1,0:T(2,128)(2,1)S(1)}, u32[]{:S(2)}, u32[]{:S(2)}) %collective-permute-start.2) | collective-permute-done | bytes 3104 | tf_op jit(solution)/shard_map/ppermute | solution.py:232
  12.2 10.3 %all-to-all-start = ((bf16[8,24,2816]{2,1,0:T(8,128)(2,1)}), bf16[8,24,2816]{2,1,0:T(8,128)(2,1)S(1)}, u32[]{:S(2)}, u32[]{:S(2)}) async-start(bf16[8,24,2816]{2,1,0:T(8,128)(2,1)} %broadcast_in_dim.25), calls=%async_computation | async-start | bytes 2162688 | tf_op jit(solution)/shard_map/all_to_all | solution.py:40
  22.6 4.1 %collective-permute-start.3 = (f32[2,768]{1,0:T(2,128)S(1)}, f32[2,768]{1,0:T(2,128)S(1)}, u32[]{:S(2)}, u32[]{:S(2)}) collective-permute-start(f32[2,768]{1,0:T(2,128)S(1)} %pad_maximum_fusion.2), channel_id=1, source_target_pairs={{0,1},{1,0},{2,3},{3,2},{4,5},{5,4},{6,7},{7,6},{8,9},{9,8},{10,11... | collective-permute-start | bytes 18440 | tf_op jit(solution)/shard_map/ppermute | solution.py:240
  27.5 6.3 %collective-permute-start.4 = (f32[2,768]{1,0:T(2,128)S(1)}, f32[2,768]{1,0:T(2,128)S(1)}, u32[]{:S(2)}, u32[]{:S(2)}) collective-permute-start(f32[2,768]{1,0:T(2,128)S(1)} %add.29), channel_id=1, source_target_pairs={{0,2},{1,3},{2,0},{3,1},{4,6},{5,7},{6,4},{7,5},{8,10},{9,11},{10,... | collective-permute-start | bytes 18440 | tf_op jit(solution)/shard_map/ppermute | solution.py:240
  35.4 9.4 %collective-permute-start.5 = (f32[2,768]{1,0:T(2,128)S(1)}, f32[2,768]{1,0:T(2,128)S(1)}, u32[]{:S(2)}, u32[]{:S(2)}) collective-permute-start(f32[2,768]{1,0:T(2,128)S(1)} %add.30), channel_id=1, source_target_pairs={{0,4},{1,5},{2,6},{3,7},{4,0},{5,1},{6,2},{7,3},{8,12},{9,13},{10,... | collective-permute-start | bytes 18440 | tf_op jit(solution)/shard_map/ppermute | solution.py:240
  46.4 3.8 %collective-permute-start.6 = (f32[2,768]{1,0:T(2,128)S(1)}, f32[2,768]{1,0:T(2,128)S(1)}, u32[]{:S(2)}, u32[]{:S(2)}) collective-permute-start(f32[2,768]{1,0:T(2,128)S(1)} %add.31), channel_id=1, source_target_pairs={{0,8},{1,9},{2,10},{3,11},{4,12},{5,13},{6,14},{7,15},{8,0},{9,1},... | collective-permute-start | bytes 18440 | tf_op jit(solution)/shard_map/ppermute | solution.py:240
  50.3 5.6 %collective-permute-done.6 = f32[2,768]{1,0:T(2,128)S(1)} collective-permute-done((f32[2,768]{1,0:T(2,128)S(1)}, f32[2,768]{1,0:T(2,128)S(1)}, u32[]{:S(2)}, u32[]{:S(2)}) %collective-permute-start.6) | collective-permute-done | bytes 6176 | tf_op jit(solution)/shard_map/ppermute | solution.py:240
  55.8 1.9 %collective-permute-start.10 = (bf16[8,24,2816]{2,1,0:T(8,128)(2,1)S(1)}, bf16[8,24,2816]{2,1,0:T(8,128)(2,1)S(1)}, u32[]{:S(2)}, u32[]{:S(2)}) collective-permute-start(bf16[8,24,2816]{2,1,0:T(8,128)(2,1)S(1)} %all-to-all-done), channel_id=1, source_target_pairs={{0,1},{1,0},{2,3},{3,2},{4,5},{5,4},{6,7},{7,6},{8,9},{9,8},{10,11... | collective-permute-start | bytes 3244040 | tf_op jit(solution)/shard_map/ppermute | solution.py:244
  57.8 3.9 %collective-permute-start.7 = (bf16[288,768]{1,0:T(8,128)(2,1)S(1)}, bf16[288,768]{1,0:T(8,128)(2,1)}, u32[]{:S(2)}, u32[]{:S(2)}) collective-permute-start(bf16[288,768]{1,0:T(8,128)(2,1)S(1)} %concatenate.10.x0), channel_id=1, source_target_pairs={{0,2},{1,3},{2,4},{3,5},{4,6},{5,7},{6,0},{7,1},{8,10},{9,11},{10,... | collective-permute-start | bytes 1327112 | tf_op jit(solution)/shard_map/ppermute | solution.py:242
  61.7 5.5 %collective-permute-start.8 = (bf16[288,768]{1,0:T(8,128)(2,1)S(1)}, bf16[288,768]{1,0:T(8,128)(2,1)}, u32[]{:S(2)}, u32[]{:S(2)}) collective-permute-start(bf16[288,768]{1,0:T(8,128)(2,1)S(1)} %concatenate.10.x0), channel_id=1, source_target_pairs={{0,4},{1,5},{2,6},{3,7},{4,0},{5,1},{6,2},{7,3},{8,12},{9,13},{10,... | collective-permute-start | bytes 1327112 | tf_op jit(solution)/shard_map/ppermute | solution.py:242
  67.1 2.5 %collective-permute-start.9 = (bf16[288,768]{1,0:T(8,128)(2,1)S(1)}, bf16[288,768]{1,0:T(8,128)(2,1)}, u32[]{:S(2)}, u32[]{:S(2)}) collective-permute-start(bf16[288,768]{1,0:T(8,128)(2,1)S(1)} %concatenate.10.x0), channel_id=1, source_target_pairs={{0,6},{1,7},{2,0},{3,1},{4,2},{5,3},{6,4},{7,5},{8,14},{9,15},{10,... | collective-permute-start | bytes 1327112 | tf_op jit(solution)/shard_map/ppermute | solution.py:242
  70.4 9.2 %all-to-all-start.1 = ((f32[32,2,768]{2,1,0:T(2,128)}), f32[32,2,768]{2,1,0:T(2,128)}, u32[]{:S(2)}, u32[]{:S(2)}) async-start(f32[32,2,768]{2,1,0:T(2,128)} %broadcast_in_dim.26), calls=%async_computation.1 | async-start | bytes 393216 | tf_op jit(solution)/shard_map/all_to_all | solution.py:40
  79.7 3.3 %collective-permute-start.11 = (bf16[448,384]{1,0:T(8,128)(2,1)S(1)}, bf16[448,384]{1,0:T(8,128)(2,1)S(1)}, u32[]{:S(2)}, u32[]{:S(2)}) collective-permute-start(bf16[448,384]{1,0:T(8,128)(2,1)S(1)} %bitcast.44), channel_id=1, source_target_pairs={{0,2},{1,3},{2,4},{3,5},{4,6},{5,7},{6,0},{7,1},{8,10},{9,11},{10,... | collective-permute-start | bytes 1032200 | tf_op jit(solution)/shard_map/ppermute | solution.py:246
  83.1 4.2 %collective-permute-start.12 = (bf16[448,384]{1,0:T(8,128)(2,1)S(1)}, bf16[448,384]{1,0:T(8,128)(2,1)}, u32[]{:S(2)}, u32[]{:S(2)}) collective-permute-start(bf16[448,384]{1,0:T(8,128)(2,1)S(1)} %bitcast.45), channel_id=1, source_target_pairs={{0,4},{1,5},{2,6},{3,7},{4,0},{5,1},{6,2},{7,3},{8,12},{9,13},{10,... | collective-permute-start | bytes 1032200 | tf_op jit(solution)/shard_map/ppermute | solution.py:246
  87.3 2.3 %collective-permute-start.13 = (bf16[448,384]{1,0:T(8,128)(2,1)S(1)}, bf16[448,384]{1,0:T(8,128)(2,1)}, u32[]{:S(2)}, u32[]{:S(2)}) collective-permute-start(bf16[448,384]{1,0:T(8,128)(2,1)S(1)} %bitcast.46), channel_id=1, source_target_pairs={{0,6},{1,7},{2,0},{3,1},{4,2},{5,3},{6,4},{7,5},{8,14},{9,15},{10,... | collective-permute-start | bytes 1032200 | tf_op jit(solution)/shard_map/ppermute | solution.py:246
  90.9 9.0 %conv_block.1 = bf16[4,192,128]{2,1,0:T(8,128)(2,1)} custom-call(s32[4]{0:T(128)S(1)} %pad_add_fusion.where_ref, bf16[288,768]{1,0:T(8,128)(2,1)S(1)} %concatenate.10.x0, bf16[288,768]{1,0:T(8,128)(2,1)} %collective-permute-done.7.x1, bf16[288,768]{1,0:T(8,128)(2,1)} %collective-permute-done.8.x2, bf16[288,768]{1,0:T(8,128)(2,1)} %collective-permute-done.9.x3, ...), custom_call_target="tpu_custom_call" | custom-call | tf_op jit(solution)/shard_map/conv_block/pallas_call | solution.py:137
  101.9 2.2 %pad_maximum_fusion = bf16[1344,384]{1,0:T(8,128)(2,1)} fusion(bf16[448,384]{1,0:T(8,128)(2,1)} %collective-permute-done.13.refs_3_, bf16[448,384]{1,0:T(8,128)(2,1)} %collective-permute-done.12.refs_2_, bf16[448,384]{1,0:T(8,128)(2,1)S(1)} %collective-permute-done.11.refs_1_), kind=kLoop, calls=%fused_computation | loop fusion | flops 3096576 | bytes 2064384 | tf_op jit(solution)/shard_map/concatenate | solution.py:255
  106.1 3.9 %all-to-all-start.2 = ((bf16[4,192,128]{2,1,0:T(8,128)(2,1)}), bf16[4,192,128]{2,1,0:T(8,128)(2,1)S(1)}, u32[]{:S(2)}, u32[]{:S(2)}) async-start(bf16[4,192,128]{2,1,0:T(8,128)(2,1)} %conv_block.1), calls=%async_computation.2 | async-start | bytes 393216 | tf_op jit(solution)/shard_map/all_to_all | solution.py:257
  110.1 6.5 %all-to-all-done.2.part_ref = bf16[4,192,128]{2,1,0:T(8,128)(2,1)S(1)} async-done(((bf16[4,192,128]{2,1,0:T(8,128)(2,1)}), bf16[4,192,128]{2,1,0:T(8,128)(2,1)S(1)}, u32[]{:S(2)}, u32[]{:S(2)}) %all-to-all-start.2) | async-done | bytes 196640 | tf_op jit(solution)/shard_map/all_to_all | solution.py:257
  116.6 3.8 %project.1 = (bf16[128,768]{1,0:T(8,128)(2,1)}, bf16[16,224,128]{2,1,0:T(8,128)(2,1)}) custom-call(s32[4]{0:T(128)S(1)} %pad_add_fusion.where_ref, bf16[4,192,128]{2,1,0:T(8,128)(2,1)S(1)} %all-to-all-done.2.part_ref, f32[2,768]{1,0:T(2,128)S(1)} %pad_maximum_fusion.4.norm_ref, bf16[448,384]{1,0:T(8,128)(2,1)S(1)} %bitcast.47, ...), custom_call_target="tpu_custom_call" | custom-call | tf_op jit(solution)/shard_map/project/pallas_call | solution.py:191
  120.4 4.9 %all-to-all-start.3 = ((bf16[16,224,128]{2,1,0:T(8,128)(2,1)}), bf16[16,224,128]{2,1,0:T(8,128)(2,1)S(1)}, u32[]{:S(2)}, u32[]{:S(2)}) async-start(bf16[16,224,128]{2,1,0:T(8,128)(2,1)} %get-tuple-element.27), calls=%async_computation.3 | async-start | bytes 1835008 | tf_op jit(solution)/shard_map/all_to_all | solution.py:259
  125.3 28.8 %all-to-all-done.3.r_ref = bf16[16,224,128]{2,1,0:T(8,128)(2,1)S(1)} async-done(((bf16[16,224,128]{2,1,0:T(8,128)(2,1)}), bf16[16,224,128]{2,1,0:T(8,128)(2,1)S(1)}, u32[]{:S(2)}, u32[]{:S(2)}) %all-to-all-start.3) | async-done | bytes 917536 | tf_op jit(solution)/shard_map/all_to_all | solution.py:259
  154.1 4.7 %attend.1 = bf16[8,96,128]{2,1,0:T(8,128)(2,1)S(1)} custom-call(s32[1]{0:T(128)} %bitcast.21.first_ref, bf16[16,224,128]{2,1,0:T(8,128)(2,1)S(1)} %all-to-all-done.3.r_ref), custom_call_target="tpu_custom_call" | custom-call | tf_op jit(solution)/shard_map/attend/pallas_call | solution.py:67
  158.8 9.2 %all_to_all.25 = bf16[8,96,128]{2,1,0:T(8,128)(2,1)S(1)} all-to-all(bf16[8,96,128]{2,1,0:T(8,128)(2,1)S(1)} %attend.1), channel_id=1, replica_groups={{0,1,2,3,4,5,6,7},{8,9,10,11,12,13,14,15},{16,17,18,19,20,21,22,23},{24..., dimensions={0} | all-to-all | bytes 393216 | tf_op jit(solution)/shard_map/all_to_all | solution.py:261
  (64 shorter events, 18.8 us)
Async XLA Ops:
  0.6 10.2 %copy-start.1 = (bf16[1,256,768]{2,1,0:T(8,128)(2,1)S(1)}, bf16[1,256,768]{2,1,0:T(8,128)(2,1)}, u32[]{:S(2)}) copy-start(bf16[1,256,768]{2,1,0:T(8,128)(2,1)} %param.8) | copy-start | bytes 1179652
  1.6 9.5 %collective-permute-start = (bf16[24,2816]{1,0:T(8,128)(2,1)S(1)}, bf16[24,2816]{1,0:T(8,128)(2,1)S(1)}, u32[]{:S(2)}, u32[]{:S(2)}) collective-permute-start(bf16[24,2816]{1,0:T(8,128)(2,1)S(1)} %pad_maximum_fusion.1), channel_id=1, source_target_pairs={{0,0},{1,1},{130,2},{131,3},{260,4},{261,5},{398,6},{399,7},{8,8},... | collective-permute-start | bytes 405512 | tf_op jit(solution)/shard_map/ppermute | solution.py:228
  3.0 4.2 %collective-permute-start.1 = (bf16[2,768]{1,0:T(2,128)(2,1)S(1)}, bf16[2,768]{1,0:T(2,128)(2,1)S(1)}, u32[]{:S(2)}, u32[]{:S(2)}) collective-permute-start(bf16[2,768]{1,0:T(2,128)(2,1)S(1)} %get-tuple-element.31), channel_id=1, source_target_pairs={{0,1},{1,2},{2,3},{3,4},{4,5},{5,6},{6,7},{7,8},{8,9},{9,10},{10,1... | collective-permute-start | bytes 9224 | tf_op jit(solution)/shard_map/ppermute | solution.py:231
  4.8 6.0 %collective-permute-start.2 = (bf16[2,768]{1,0:T(2,128)(2,1)S(1)}, bf16[2,768]{1,0:T(2,128)(2,1)S(1)}, u32[]{:S(2)}, u32[]{:S(2)}) collective-permute-start(bf16[2,768]{1,0:T(2,128)(2,1)S(1)} %get-tuple-element.30), channel_id=1, source_target_pairs={{1,0},{2,1},{3,2},{4,3},{5,4},{6,5},{7,6},{8,7},{9,8},{10,9},{11,1... | collective-permute-start | bytes 9224 | tf_op jit(solution)/shard_map/ppermute | solution.py:232
  12.2 43.6 %all-to-all-start = ((bf16[8,24,2816]{2,1,0:T(8,128)(2,1)}), bf16[8,24,2816]{2,1,0:T(8,128)(2,1)S(1)}, u32[]{:S(2)}, u32[]{:S(2)}) async-start(bf16[8,24,2816]{2,1,0:T(8,128)(2,1)} %broadcast_in_dim.25), calls=%async_computation | async-start | bytes 2162688 | tf_op jit(solution)/shard_map/all_to_all | solution.py:40
  22.5 67.1 %copy-start.2 = (f32[768]{0:T(1024)S(1)}, f32[768]{0:T(1024)}, u32[]{:S(2)}) copy-start(f32[768]{0:T(1024)} %param.10) | copy-start | bytes 9220
  22.5 67.1 %copy-start.3 = (f32[768]{0:T(1024)S(1)}, f32[768]{0:T(1024)}, u32[]{:S(2)}) copy-start(f32[768]{0:T(1024)} %param.9) | copy-start | bytes 9220
  22.6 67.2 %copy-start.6 = (f32[768]{0:T(1024)S(1)}, f32[768]{0:T(1024)}, u32[]{:S(2)}) copy-start(f32[768]{0:T(1024)} %param.12) | copy-start | bytes 9220
  22.6 4.9 %collective-permute-start.3 = (f32[2,768]{1,0:T(2,128)S(1)}, f32[2,768]{1,0:T(2,128)S(1)}, u32[]{:S(2)}, u32[]{:S(2)}) collective-permute-start(f32[2,768]{1,0:T(2,128)S(1)} %pad_maximum_fusion.2), channel_id=1, source_target_pairs={{0,1},{1,0},{2,3},{3,2},{4,5},{5,4},{6,7},{7,6},{8,9},{9,8},{10,11... | collective-permute-start | bytes 18440 | tf_op jit(solution)/shard_map/ppermute | solution.py:240
  27.5 7.9 %collective-permute-start.4 = (f32[2,768]{1,0:T(2,128)S(1)}, f32[2,768]{1,0:T(2,128)S(1)}, u32[]{:S(2)}, u32[]{:S(2)}) collective-permute-start(f32[2,768]{1,0:T(2,128)S(1)} %add.29), channel_id=1, source_target_pairs={{0,2},{1,3},{2,0},{3,1},{4,6},{5,7},{6,4},{7,5},{8,10},{9,11},{10,... | collective-permute-start | bytes 18440 | tf_op jit(solution)/shard_map/ppermute | solution.py:240
  35.4 11.0 %collective-permute-start.5 = (f32[2,768]{1,0:T(2,128)S(1)}, f32[2,768]{1,0:T(2,128)S(1)}, u32[]{:S(2)}, u32[]{:S(2)}) collective-permute-start(f32[2,768]{1,0:T(2,128)S(1)} %add.30), channel_id=1, source_target_pairs={{0,4},{1,5},{2,6},{3,7},{4,0},{5,1},{6,2},{7,3},{8,12},{9,13},{10,... | collective-permute-start | bytes 18440 | tf_op jit(solution)/shard_map/ppermute | solution.py:240
  46.4 9.4 %collective-permute-start.6 = (f32[2,768]{1,0:T(2,128)S(1)}, f32[2,768]{1,0:T(2,128)S(1)}, u32[]{:S(2)}, u32[]{:S(2)}) collective-permute-start(f32[2,768]{1,0:T(2,128)S(1)} %add.31), channel_id=1, source_target_pairs={{0,8},{1,9},{2,10},{3,11},{4,12},{5,13},{6,14},{7,15},{8,0},{9,1},... | collective-permute-start | bytes 18440 | tf_op jit(solution)/shard_map/ppermute | solution.py:240
  55.8 35.1 %collective-permute-start.10 = (bf16[8,24,2816]{2,1,0:T(8,128)(2,1)S(1)}, bf16[8,24,2816]{2,1,0:T(8,128)(2,1)S(1)}, u32[]{:S(2)}, u32[]{:S(2)}) collective-permute-start(bf16[8,24,2816]{2,1,0:T(8,128)(2,1)S(1)} %all-to-all-done), channel_id=1, source_target_pairs={{0,1},{1,0},{2,3},{3,2},{4,5},{5,4},{6,7},{7,6},{8,9},{9,8},{10,11... | collective-permute-start | bytes 3244040 | tf_op jit(solution)/shard_map/ppermute | solution.py:244
  57.8 25.3 %collective-permute-start.7 = (bf16[288,768]{1,0:T(8,128)(2,1)S(1)}, bf16[288,768]{1,0:T(8,128)(2,1)}, u32[]{:S(2)}, u32[]{:S(2)}) collective-permute-start(bf16[288,768]{1,0:T(8,128)(2,1)S(1)} %concatenate.10.x0), channel_id=1, source_target_pairs={{0,2},{1,3},{2,4},{3,5},{4,6},{5,7},{6,0},{7,1},{8,10},{9,11},{10,... | collective-permute-start | bytes 1327112 | tf_op jit(solution)/shard_map/ppermute | solution.py:242
  61.7 25.6 %collective-permute-start.8 = (bf16[288,768]{1,0:T(8,128)(2,1)S(1)}, bf16[288,768]{1,0:T(8,128)(2,1)}, u32[]{:S(2)}, u32[]{:S(2)}) collective-permute-start(bf16[288,768]{1,0:T(8,128)(2,1)S(1)} %concatenate.10.x0), channel_id=1, source_target_pairs={{0,4},{1,5},{2,6},{3,7},{4,0},{5,1},{6,2},{7,3},{8,12},{9,13},{10,... | collective-permute-start | bytes 1327112 | tf_op jit(solution)/shard_map/ppermute | solution.py:242
  67.1 23.8 %collective-permute-start.9 = (bf16[288,768]{1,0:T(8,128)(2,1)S(1)}, bf16[288,768]{1,0:T(8,128)(2,1)}, u32[]{:S(2)}, u32[]{:S(2)}) collective-permute-start(bf16[288,768]{1,0:T(8,128)(2,1)S(1)} %concatenate.10.x0), channel_id=1, source_target_pairs={{0,6},{1,7},{2,0},{3,1},{4,2},{5,3},{6,4},{7,5},{8,14},{9,15},{10,... | collective-permute-start | bytes 1327112 | tf_op jit(solution)/shard_map/ppermute | solution.py:242
  70.4 19.5 %all-to-all-start.1 = ((f32[32,2,768]{2,1,0:T(2,128)}), f32[32,2,768]{2,1,0:T(2,128)}, u32[]{:S(2)}, u32[]{:S(2)}) async-start(f32[32,2,768]{2,1,0:T(2,128)} %broadcast_in_dim.26), calls=%async_computation.1 | async-start | bytes 393216 | tf_op jit(solution)/shard_map/all_to_all | solution.py:40
  79.7 20.2 %collective-permute-start.11 = (bf16[448,384]{1,0:T(8,128)(2,1)S(1)}, bf16[448,384]{1,0:T(8,128)(2,1)S(1)}, u32[]{:S(2)}, u32[]{:S(2)}) collective-permute-start(bf16[448,384]{1,0:T(8,128)(2,1)S(1)} %bitcast.44), channel_id=1, source_target_pairs={{0,2},{1,3},{2,4},{3,5},{4,6},{5,7},{6,0},{7,1},{8,10},{9,11},{10,... | collective-permute-start | bytes 1032200 | tf_op jit(solution)/shard_map/ppermute | solution.py:246
  83.1 17.0 %collective-permute-start.12 = (bf16[448,384]{1,0:T(8,128)(2,1)S(1)}, bf16[448,384]{1,0:T(8,128)(2,1)}, u32[]{:S(2)}, u32[]{:S(2)}) collective-permute-start(bf16[448,384]{1,0:T(8,128)(2,1)S(1)} %bitcast.45), channel_id=1, source_target_pairs={{0,4},{1,5},{2,6},{3,7},{4,0},{5,1},{6,2},{7,3},{8,12},{9,13},{10,... | collective-permute-start | bytes 1032200 | tf_op jit(solution)/shard_map/ppermute | solution.py:246
  87.3 14.7 %collective-permute-start.13 = (bf16[448,384]{1,0:T(8,128)(2,1)S(1)}, bf16[448,384]{1,0:T(8,128)(2,1)}, u32[]{:S(2)}, u32[]{:S(2)}) collective-permute-start(bf16[448,384]{1,0:T(8,128)(2,1)S(1)} %bitcast.46), channel_id=1, source_target_pairs={{0,6},{1,7},{2,0},{3,1},{4,2},{5,3},{6,4},{7,5},{8,14},{9,15},{10,... | collective-permute-start | bytes 1032200 | tf_op jit(solution)/shard_map/ppermute | solution.py:246
  100.0 6.1 %copy-start.5 = (f32[768]{0:T(1024)S(1)}, f32[768]{0:T(1024)}, u32[]{:S(2)}) copy-start(f32[768]{0:T(1024)} %param.13) | copy-start | bytes 9220
  104.1 12.5 %collective-permute-start.14 = (bf16[1344,384]{1,0:T(8,128)(2,1)}, bf16[1344,384]{1,0:T(8,128)(2,1)}, u32[]{:S(2)}, u32[]{:S(2)}) collective-permute-start(bf16[1344,384]{1,0:T(8,128)(2,1)} %pad_maximum_fusion), channel_id=1, source_target_pairs={{0,1},{1,0},{2,3},{3,2},{4,5},{5,4},{6,7},{7,6},{8,9},{9,8},{10,11... | collective-permute-start | bytes 3096584 | tf_op jit(solution)/shard_map/ppermute | solution.py:255
  106.1 10.5 %all-to-all-start.2 = ((bf16[4,192,128]{2,1,0:T(8,128)(2,1)}), bf16[4,192,128]{2,1,0:T(8,128)(2,1)S(1)}, u32[]{:S(2)}, u32[]{:S(2)}) async-start(bf16[4,192,128]{2,1,0:T(8,128)(2,1)} %conv_block.1), calls=%async_computation.2 | async-start | bytes 393216 | tf_op jit(solution)/shard_map/all_to_all | solution.py:257
  120.4 33.7 %all-to-all-start.3 = ((bf16[16,224,128]{2,1,0:T(8,128)(2,1)}), bf16[16,224,128]{2,1,0:T(8,128)(2,1)S(1)}, u32[]{:S(2)}, u32[]{:S(2)}) async-start(bf16[16,224,128]{2,1,0:T(8,128)(2,1)} %get-tuple-element.27), calls=%async_computation.3 | async-start | bytes 1835008 | tf_op jit(solution)/shard_map/all_to_all | solution.py:259
  (2 other events, 7.0 us)

commit v4 on v3

--- a/solution.py
+++ b/solution.py
@@ -81,8 +81,9 @@
                 out_ref, act, product, *, count):
     core, x_at, y_hi = where_ref[0], where_ref[1], where_ref[2]
     bias = bias_ref[pl.ds(lax.rem(x_at + where_ref[3], 4), 1)]
-    mean = sums_ref[0:1] / count
-    scale = lax.rsqrt(sums_ref[1:2] / count - mean * mean + epsilon) * norm_ref[0:1]
+    sums = jnp.sum(sums_ref[...], axis=0)
+    mean = sums[0:1] / count
+    scale = lax.rsqrt(sums[1:2] / count - mean * mean + epsilon) * norm_ref[0:1]
     shift = norm_ref[1:2]
     near = pl.multiple_of(core * 384, 128)
     far = pl.multiple_of(384 - core * 384, 128)
@@ -244,7 +245,7 @@
     other = lax.ppermute(mine, "seq", swap)
     own = qkv_rows(mine)
     near = [lax.ppermute(own, "seq", x_shift(k)) for k in range(1, 4)]
-    sums = jnp.sum(to_all(sums, "batch"), axis=0)
+    sums = to_all(sums, "batch")
     count = float(raw.shape[0] * lax.axis_size("batch") * lax.axis_size("seq"))
 
     part = conv_block(

time: 170 us -> 170 us (level)
  transfers between devices with their start and end apart: 19 -> 19, of which waited for: 9 -> 9; matrix products, arithmetic and copies ran while one was open for 3% -> 2% of each run, Pallas kernels for 5% -> 5%
where the time goes in v4:
time: 170 us; the launch traced here: 169 us
  starting transfers between devices  81.2 us (48%)
  waiting for transfers between devices  51.3 us (30%)
  Pallas kernels  17.6 us (10%)
  blocking collectives  9.23 us (5%)
  local copies, waits for them, and re-layouts  4.9 us (3%)
  other arithmetic  3.41 us (2%)
    all_to_all x1, waiting for transfers between devices, on_device(): packed = lax.all_to_all(packed, 'seq', 0, 0, tiled=True)  28.8 us
    ppermute x4, starting transfers between devices, on_device(): sums = sums + lax.ppermute(sums, 'seq', [(i, i ^ bit) for i in range(16)])  23.7 us
    all_to_all x2, starting transfers between devices, to_all(): lax.all_to_all(jnp.broadcast_to(values[None], (count,) + values.shape), a...  19.6 us
    ppermute x3, starting transfers between devices, on_device(): lax.ppermute(block, 'seq', x_shift(k))  11.9 us
    ppermute x3, starting transfers between devices, on_device(): near = [lax.ppermute(own, 'seq', x_shift(k)) for k in range(1, 4)]  9.82 us
    ppermute x4, waiting for transfers between devices, on_device(): sums = sums + lax.ppermute(sums, 'seq', [(i, i ^ bit) for i in range(16)])  9.56 us
    all_to_all x1, blocking collectives, on_device(): lax.all_to_all(out, 'seq', 0, 0, axis_index_groups=HALF_GROUPS, tiled=True)  9.23 us
    pallas_call x1, Pallas kernels, conv_block(): pl.pallas_call(functools.partial(conv_kernel, count=count), out_shape=jax...  9.17 us
  transfers between devices with their start and end apart: 19, of which 9 were waited for; matrix products, arithmetic and copies ran while one was open for 2% of the time, Pallas kernels for 5%

profile of v4, /device:TPU:8, one launch (start us, length us, event | category | flops | bytes accessed | tf_op | source)
XLA Modules:
  0.0 168.8 jit_solution(4229251380703831931)
XLA Ops:
  7.2 3.6 %collective-permute-done.2 = bf16[2,768]{1,0:T(2,128)(2,1)S(1)} collective-permute-done((bf16[2,768]{1,0:T(2,128)(2,1)S(1)}, bf16[2,768]{1,0:T(2,128)(2,1)S(1)}, u32[]{:S(2)}, u32[]{:S(2)}) %collective-permute-start.2) | collective-permute-done | bytes 3104 | tf_op jit(solution)/shard_map/ppermute | solution.py:233
  12.2 10.3 %all-to-all-start = ((bf16[8,24,2816]{2,1,0:T(8,128)(2,1)}), bf16[8,24,2816]{2,1,0:T(8,128)(2,1)S(1)}, u32[]{:S(2)}, u32[]{:S(2)}) async-start(bf16[8,24,2816]{2,1,0:T(8,128)(2,1)} %broadcast_in_dim.25), calls=%async_computation | async-start | bytes 2162688 | tf_op jit(solution)/shard_map/all_to_all | solution.py:40
  22.5 4.1 %collective-permute-start.3 = (f32[2,768]{1,0:T(2,128)S(1)}, f32[2,768]{1,0:T(2,128)S(1)}, u32[]{:S(2)}, u32[]{:S(2)}) collective-permute-start(f32[2,768]{1,0:T(2,128)S(1)} %pad_maximum_fusion.2), channel_id=1, source_target_pairs={{0,1},{1,0},{2,3},{3,2},{4,5},{5,4},{6,7},{7,6},{8,9},{9,8},{10,11... | collective-permute-start | bytes 18440 | tf_op jit(solution)/shard_map/ppermute | solution.py:241
  27.5 6.3 %collective-permute-start.4 = (f32[2,768]{1,0:T(2,128)S(1)}, f32[2,768]{1,0:T(2,128)S(1)}, u32[]{:S(2)}, u32[]{:S(2)}) collective-permute-start(f32[2,768]{1,0:T(2,128)S(1)} %add.29), channel_id=1, source_target_pairs={{0,2},{1,3},{2,0},{3,1},{4,6},{5,7},{6,4},{7,5},{8,10},{9,11},{10,... | collective-permute-start | bytes 18440 | tf_op jit(solution)/shard_map/ppermute | solution.py:241
  35.4 9.4 %collective-permute-start.5 = (f32[2,768]{1,0:T(2,128)S(1)}, f32[2,768]{1,0:T(2,128)S(1)}, u32[]{:S(2)}, u32[]{:S(2)}) collective-permute-start(f32[2,768]{1,0:T(2,128)S(1)} %add.30), channel_id=1, source_target_pairs={{0,4},{1,5},{2,6},{3,7},{4,0},{5,1},{6,2},{7,3},{8,12},{9,13},{10,... | collective-permute-start | bytes 18440 | tf_op jit(solution)/shard_map/ppermute | solution.py:241
  46.4 3.8 %collective-permute-start.6 = (f32[2,768]{1,0:T(2,128)S(1)}, f32[2,768]{1,0:T(2,128)S(1)}, u32[]{:S(2)}, u32[]{:S(2)}) collective-permute-start(f32[2,768]{1,0:T(2,128)S(1)} %add.31), channel_id=1, source_target_pairs={{0,8},{1,9},{2,10},{3,11},{4,12},{5,13},{6,14},{7,15},{8,0},{9,1},... | collective-permute-start | bytes 18440 | tf_op jit(solution)/shard_map/ppermute | solution.py:241
  50.2 5.6 %collective-permute-done.6 = f32[2,768]{1,0:T(2,128)S(1)} collective-permute-done((f32[2,768]{1,0:T(2,128)S(1)}, f32[2,768]{1,0:T(2,128)S(1)}, u32[]{:S(2)}, u32[]{:S(2)}) %collective-permute-start.6) | collective-permute-done | bytes 6176 | tf_op jit(solution)/shard_map/ppermute | solution.py:241
  55.8 1.9 %collective-permute-start.10 = (bf16[8,24,2816]{2,1,0:T(8,128)(2,1)S(1)}, bf16[8,24,2816]{2,1,0:T(8,128)(2,1)S(1)}, u32[]{:S(2)}, u32[]{:S(2)}) collective-permute-start(bf16[8,24,2816]{2,1,0:T(8,128)(2,1)S(1)} %all-to-all-done), channel_id=1, source_target_pairs={{0,1},{1,0},{2,3},{3,2},{4,5},{5,4},{6,7},{7,6},{8,9},{9,8},{10,11... | collective-permute-start | bytes 3244040 | tf_op jit(solution)/shard_map/ppermute | solution.py:245
  57.7 3.9 %collective-permute-start.7 = (bf16[288,768]{1,0:T(8,128)(2,1)S(1)}, bf16[288,768]{1,0:T(8,128)(2,1)}, u32[]{:S(2)}, u32[]{:S(2)}) collective-permute-start(bf16[288,768]{1,0:T(8,128)(2,1)S(1)} %concatenate.10.x0), channel_id=1, source_target_pairs={{0,2},{1,3},{2,4},{3,5},{4,6},{5,7},{6,0},{7,1},{8,10},{9,11},{10,... | collective-permute-start | bytes 1327112 | tf_op jit(solution)/shard_map/ppermute | solution.py:243
  61.6 5.5 %collective-permute-start.8 = (bf16[288,768]{1,0:T(8,128)(2,1)S(1)}, bf16[288,768]{1,0:T(8,128)(2,1)}, u32[]{:S(2)}, u32[]{:S(2)}) collective-permute-start(bf16[288,768]{1,0:T(8,128)(2,1)S(1)} %concatenate.10.x0), channel_id=1, source_target_pairs={{0,4},{1,5},{2,6},{3,7},{4,0},{5,1},{6,2},{7,3},{8,12},{9,13},{10,... | collective-permute-start | bytes 1327112 | tf_op jit(solution)/shard_map/ppermute | solution.py:243
  67.1 2.5 %collective-permute-start.9 = (bf16[288,768]{1,0:T(8,128)(2,1)S(1)}, bf16[288,768]{1,0:T(8,128)(2,1)}, u32[]{:S(2)}, u32[]{:S(2)}) collective-permute-start(bf16[288,768]{1,0:T(8,128)(2,1)S(1)} %concatenate.10.x0), channel_id=1, source_target_pairs={{0,6},{1,7},{2,0},{3,1},{4,2},{5,3},{6,4},{7,5},{8,14},{9,15},{10,... | collective-permute-start | bytes 1327112 | tf_op jit(solution)/shard_map/ppermute | solution.py:243
  70.4 9.2 %all-to-all-start.1 = ((f32[32,2,768]{2,1,0:T(2,128)}), f32[32,2,768]{2,1,0:T(2,128)}, u32[]{:S(2)}, u32[]{:S(2)}) async-start(f32[32,2,768]{2,1,0:T(2,128)} %broadcast_in_dim.26), calls=%async_computation.1 | async-start | bytes 393216 | tf_op jit(solution)/shard_map/all_to_all | solution.py:40
  79.7 3.3 %collective-permute-start.11 = (bf16[448,384]{1,0:T(8,128)(2,1)S(1)}, bf16[448,384]{1,0:T(8,128)(2,1)S(1)}, u32[]{:S(2)}, u32[]{:S(2)}) collective-permute-start(bf16[448,384]{1,0:T(8,128)(2,1)S(1)} %bitcast.44), channel_id=1, source_target_pairs={{0,2},{1,3},{2,4},{3,5},{4,6},{5,7},{6,0},{7,1},{8,10},{9,11},{10,... | collective-permute-start | bytes 1032200 | tf_op jit(solution)/shard_map/ppermute | solution.py:247
  83.1 4.2 %collective-permute-start.12 = (bf16[448,384]{1,0:T(8,128)(2,1)S(1)}, bf16[448,384]{1,0:T(8,128)(2,1)}, u32[]{:S(2)}, u32[]{:S(2)}) collective-permute-start(bf16[448,384]{1,0:T(8,128)(2,1)S(1)} %bitcast.45), channel_id=1, source_target_pairs={{0,4},{1,5},{2,6},{3,7},{4,0},{5,1},{6,2},{7,3},{8,12},{9,13},{10,... | collective-permute-start | bytes 1032200 | tf_op jit(solution)/shard_map/ppermute | solution.py:247
  87.2 2.3 %collective-permute-start.13 = (bf16[448,384]{1,0:T(8,128)(2,1)S(1)}, bf16[448,384]{1,0:T(8,128)(2,1)}, u32[]{:S(2)}, u32[]{:S(2)}) collective-permute-start(bf16[448,384]{1,0:T(8,128)(2,1)S(1)} %bitcast.46), channel_id=1, source_target_pairs={{0,6},{1,7},{2,0},{3,1},{4,2},{5,3},{6,4},{7,5},{8,14},{9,15},{10,... | collective-permute-start | bytes 1032200 | tf_op jit(solution)/shard_map/ppermute | solution.py:247
  89.9 9.2 %conv_block.1 = bf16[4,192,128]{2,1,0:T(8,128)(2,1)} custom-call(s32[4]{0:T(128)S(1)} %pad_add_fusion.where_ref, bf16[288,768]{1,0:T(8,128)(2,1)S(1)} %concatenate.10.x0, bf16[288,768]{1,0:T(8,128)(2,1)} %collective-permute-done.7.x1, bf16[288,768]{1,0:T(8,128)(2,1)} %collective-permute-done.8.x2, bf16[288,768]{1,0:T(8,128)(2,1)} %collective-permute-done.9.x3, ...), custom_call_target="tpu_custom_call" | custom-call | tf_op jit(solution)/shard_map/conv_block/pallas_call | solution.py:138
  101.9 2.2 %pad_maximum_fusion = bf16[1344,384]{1,0:T(8,128)(2,1)} fusion(bf16[448,384]{1,0:T(8,128)(2,1)} %collective-permute-done.13.refs_3_, bf16[448,384]{1,0:T(8,128)(2,1)} %collective-permute-done.12.refs_2_, bf16[448,384]{1,0:T(8,128)(2,1)S(1)} %collective-permute-done.11.refs_1_), kind=kLoop, calls=%fused_computation | loop fusion | flops 3096576 | bytes 2064384 | tf_op jit(solution)/shard_map/concatenate | solution.py:256
  106.1 3.9 %all-to-all-start.2 = ((bf16[4,192,128]{2,1,0:T(8,128)(2,1)}), bf16[4,192,128]{2,1,0:T(8,128)(2,1)S(1)}, u32[]{:S(2)}, u32[]{:S(2)}) async-start(bf16[4,192,128]{2,1,0:T(8,128)(2,1)} %conv_block.1), calls=%async_computation.2 | async-start | bytes 393216 | tf_op jit(solution)/shard_map/all_to_all | solution.py:258
  110.1 6.5 %all-to-all-done.2.part_ref = bf16[4,192,128]{2,1,0:T(8,128)(2,1)S(1)} async-done(((bf16[4,192,128]{2,1,0:T(8,128)(2,1)}), bf16[4,192,128]{2,1,0:T(8,128)(2,1)S(1)}, u32[]{:S(2)}, u32[]{:S(2)}) %all-to-all-start.2) | async-done | bytes 196640 | tf_op jit(solution)/shard_map/all_to_all | solution.py:258
  116.6 3.8 %project.1 = (bf16[128,768]{1,0:T(8,128)(2,1)}, bf16[16,224,128]{2,1,0:T(8,128)(2,1)}) custom-call(s32[4]{0:T(128)S(1)} %pad_add_fusion.where_ref, bf16[4,192,128]{2,1,0:T(8,128)(2,1)S(1)} %all-to-all-done.2.part_ref, f32[2,768]{1,0:T(2,128)S(1)} %pad_maximum_fusion.4.norm_ref, bf16[448,384]{1,0:T(8,128)(2,1)S(1)} %bitcast.47, ...), custom_call_target="tpu_custom_call" | custom-call | tf_op jit(solution)/shard_map/project/pallas_call | solution.py:192
  120.4 4.9 %all-to-all-start.3 = ((bf16[16,224,128]{2,1,0:T(8,128)(2,1)}), bf16[16,224,128]{2,1,0:T(8,128)(2,1)S(1)}, u32[]{:S(2)}, u32[]{:S(2)}) async-start(bf16[16,224,128]{2,1,0:T(8,128)(2,1)} %get-tuple-element.27), calls=%async_computation.3 | async-start | bytes 1835008 | tf_op jit(solution)/shard_map/all_to_all | solution.py:260
  125.2 28.8 %all-to-all-done.3.r_ref = bf16[16,224,128]{2,1,0:T(8,128)(2,1)S(1)} async-done(((bf16[16,224,128]{2,1,0:T(8,128)(2,1)}), bf16[16,224,128]{2,1,0:T(8,128)(2,1)S(1)}, u32[]{:S(2)}, u32[]{:S(2)}) %all-to-all-start.3) | async-done | bytes 917536 | tf_op jit(solution)/shard_map/all_to_all | solution.py:260
  154.1 4.7 %attend.1 = bf16[8,96,128]{2,1,0:T(8,128)(2,1)S(1)} custom-call(s32[1]{0:T(128)} %bitcast.21.first_ref, bf16[16,224,128]{2,1,0:T(8,128)(2,1)S(1)} %all-to-all-done.3.r_ref), custom_call_target="tpu_custom_call" | custom-call | tf_op jit(solution)/shard_map/attend/pallas_call | solution.py:67
  158.8 9.2 %all_to_all.25 = bf16[8,96,128]{2,1,0:T(8,128)(2,1)S(1)} all-to-all(bf16[8,96,128]{2,1,0:T(8,128)(2,1)S(1)} %attend.1), channel_id=1, replica_groups={{0,1,2,3,4,5,6,7},{8,9,10,11,12,13,14,15},{16,17,18,19,20,21,22,23},{24..., dimensions={0} | all-to-all | bytes 393216 | tf_op jit(solution)/shard_map/all_to_all | solution.py:262
  (63 shorter events, 18.6 us)
Async XLA Ops:
  0.6 10.2 %copy-start.1 = (bf16[1,256,768]{2,1,0:T(8,128)(2,1)S(1)}, bf16[1,256,768]{2,1,0:T(8,128)(2,1)}, u32[]{:S(2)}) copy-start(bf16[1,256,768]{2,1,0:T(8,128)(2,1)} %param.8) | copy-start | bytes 1179652
  1.6 9.5 %collective-permute-start = (bf16[24,2816]{1,0:T(8,128)(2,1)S(1)}, bf16[24,2816]{1,0:T(8,128)(2,1)S(1)}, u32[]{:S(2)}, u32[]{:S(2)}) collective-permute-start(bf16[24,2816]{1,0:T(8,128)(2,1)S(1)} %pad_maximum_fusion.1), channel_id=1, source_target_pairs={{0,0},{1,1},{130,2},{131,3},{260,4},{261,5},{398,6},{399,7},{8,8},... | collective-permute-start | bytes 405512 | tf_op jit(solution)/shard_map/ppermute | solution.py:229
  3.0 4.2 %collective-permute-start.1 = (bf16[2,768]{1,0:T(2,128)(2,1)S(1)}, bf16[2,768]{1,0:T(2,128)(2,1)S(1)}, u32[]{:S(2)}, u32[]{:S(2)}) collective-permute-start(bf16[2,768]{1,0:T(2,128)(2,1)S(1)} %get-tuple-element.31), channel_id=1, source_target_pairs={{0,1},{1,2},{2,3},{3,4},{4,5},{5,6},{6,7},{7,8},{8,9},{9,10},{10,1... | collective-permute-start | bytes 9224 | tf_op jit(solution)/shard_map/ppermute | solution.py:232
  4.8 6.0 %collective-permute-start.2 = (bf16[2,768]{1,0:T(2,128)(2,1)S(1)}, bf16[2,768]{1,0:T(2,128)(2,1)S(1)}, u32[]{:S(2)}, u32[]{:S(2)}) collective-permute-start(bf16[2,768]{1,0:T(2,128)(2,1)S(1)} %get-tuple-element.30), channel_id=1, source_target_pairs={{1,0},{2,1},{3,2},{4,3},{5,4},{6,5},{7,6},{8,7},{9,8},{10,9},{11,1... | collective-permute-start | bytes 9224 | tf_op jit(solution)/shard_map/ppermute | solution.py:233
  12.2 43.6 %all-to-all-start = ((bf16[8,24,2816]{2,1,0:T(8,128)(2,1)}), bf16[8,24,2816]{2,1,0:T(8,128)(2,1)S(1)}, u32[]{:S(2)}, u32[]{:S(2)}) async-start(bf16[8,24,2816]{2,1,0:T(8,128)(2,1)} %broadcast_in_dim.25), calls=%async_computation | async-start | bytes 2162688 | tf_op jit(solution)/shard_map/all_to_all | solution.py:40
  22.5 67.1 %copy-start.2 = (f32[768]{0:T(1024)S(1)}, f32[768]{0:T(1024)}, u32[]{:S(2)}) copy-start(f32[768]{0:T(1024)} %param.10) | copy-start | bytes 9220
  22.5 67.1 %copy-start.3 = (f32[768]{0:T(1024)S(1)}, f32[768]{0:T(1024)}, u32[]{:S(2)}) copy-start(f32[768]{0:T(1024)} %param.9) | copy-start | bytes 9220
  22.5 67.2 %copy-start.6 = (f32[768]{0:T(1024)S(1)}, f32[768]{0:T(1024)}, u32[]{:S(2)}) copy-start(f32[768]{0:T(1024)} %param.12) | copy-start | bytes 9220
  22.5 4.9 %collective-permute-start.3 = (f32[2,768]{1,0:T(2,128)S(1)}, f32[2,768]{1,0:T(2,128)S(1)}, u32[]{:S(2)}, u32[]{:S(2)}) collective-permute-start(f32[2,768]{1,0:T(2,128)S(1)} %pad_maximum_fusion.2), channel_id=1, source_target_pairs={{0,1},{1,0},{2,3},{3,2},{4,5},{5,4},{6,7},{7,6},{8,9},{9,8},{10,11... | collective-permute-start | bytes 18440 | tf_op jit(solution)/shard_map/ppermute | solution.py:241
  27.5 7.9 %collective-permute-start.4 = (f32[2,768]{1,0:T(2,128)S(1)}, f32[2,768]{1,0:T(2,128)S(1)}, u32[]{:S(2)}, u32[]{:S(2)}) collective-permute-start(f32[2,768]{1,0:T(2,128)S(1)} %add.29), channel_id=1, source_target_pairs={{0,2},{1,3},{2,0},{3,1},{4,6},{5,7},{6,4},{7,5},{8,10},{9,11},{10,... | collective-permute-start | bytes 18440 | tf_op jit(solution)/shard_map/ppermute | solution.py:241
  35.4 11.0 %collective-permute-start.5 = (f32[2,768]{1,0:T(2,128)S(1)}, f32[2,768]{1,0:T(2,128)S(1)}, u32[]{:S(2)}, u32[]{:S(2)}) collective-permute-start(f32[2,768]{1,0:T(2,128)S(1)} %add.30), channel_id=1, source_target_pairs={{0,4},{1,5},{2,6},{3,7},{4,0},{5,1},{6,2},{7,3},{8,12},{9,13},{10,... | collective-permute-start | bytes 18440 | tf_op jit(solution)/shard_map/ppermute | solution.py:241
  46.4 9.4 %collective-permute-start.6 = (f32[2,768]{1,0:T(2,128)S(1)}, f32[2,768]{1,0:T(2,128)S(1)}, u32[]{:S(2)}, u32[]{:S(2)}) collective-permute-start(f32[2,768]{1,0:T(2,128)S(1)} %add.31), channel_id=1, source_target_pairs={{0,8},{1,9},{2,10},{3,11},{4,12},{5,13},{6,14},{7,15},{8,0},{9,1},... | collective-permute-start | bytes 18440 | tf_op jit(solution)/shard_map/ppermute | solution.py:241
  55.8 34.1 %collective-permute-start.10 = (bf16[8,24,2816]{2,1,0:T(8,128)(2,1)S(1)}, bf16[8,24,2816]{2,1,0:T(8,128)(2,1)S(1)}, u32[]{:S(2)}, u32[]{:S(2)}) collective-permute-start(bf16[8,24,2816]{2,1,0:T(8,128)(2,1)S(1)} %all-to-all-done), channel_id=1, source_target_pairs={{0,1},{1,0},{2,3},{3,2},{4,5},{5,4},{6,7},{7,6},{8,9},{9,8},{10,11... | collective-permute-start | bytes 3244040 | tf_op jit(solution)/shard_map/ppermute | solution.py:245
  57.7 25.3 %collective-permute-start.7 = (bf16[288,768]{1,0:T(8,128)(2,1)S(1)}, bf16[288,768]{1,0:T(8,128)(2,1)}, u32[]{:S(2)}, u32[]{:S(2)}) collective-permute-start(bf16[288,768]{1,0:T(8,128)(2,1)S(1)} %concatenate.10.x0), channel_id=1, source_target_pairs={{0,2},{1,3},{2,4},{3,5},{4,6},{5,7},{6,0},{7,1},{8,10},{9,11},{10,... | collective-permute-start | bytes 1327112 | tf_op jit(solution)/shard_map/ppermute | solution.py:243
  61.6 25.6 %collective-permute-start.8 = (bf16[288,768]{1,0:T(8,128)(2,1)S(1)}, bf16[288,768]{1,0:T(8,128)(2,1)}, u32[]{:S(2)}, u32[]{:S(2)}) collective-permute-start(bf16[288,768]{1,0:T(8,128)(2,1)S(1)} %concatenate.10.x0), channel_id=1, source_target_pairs={{0,4},{1,5},{2,6},{3,7},{4,0},{5,1},{6,2},{7,3},{8,12},{9,13},{10,... | collective-permute-start | bytes 1327112 | tf_op jit(solution)/shard_map/ppermute | solution.py:243
  67.1 22.8 %collective-permute-start.9 = (bf16[288,768]{1,0:T(8,128)(2,1)S(1)}, bf16[288,768]{1,0:T(8,128)(2,1)}, u32[]{:S(2)}, u32[]{:S(2)}) collective-permute-start(bf16[288,768]{1,0:T(8,128)(2,1)S(1)} %concatenate.10.x0), channel_id=1, source_target_pairs={{0,6},{1,7},{2,0},{3,1},{4,2},{5,3},{6,4},{7,5},{8,14},{9,15},{10,... | collective-permute-start | bytes 1327112 | tf_op jit(solution)/shard_map/ppermute | solution.py:243
  70.4 19.5 %all-to-all-start.1 = ((f32[32,2,768]{2,1,0:T(2,128)}), f32[32,2,768]{2,1,0:T(2,128)}, u32[]{:S(2)}, u32[]{:S(2)}) async-start(f32[32,2,768]{2,1,0:T(2,128)} %broadcast_in_dim.26), calls=%async_computation.1 | async-start | bytes 393216 | tf_op jit(solution)/shard_map/all_to_all | solution.py:40
  79.7 19.4 %collective-permute-start.11 = (bf16[448,384]{1,0:T(8,128)(2,1)S(1)}, bf16[448,384]{1,0:T(8,128)(2,1)S(1)}, u32[]{:S(2)}, u32[]{:S(2)}) collective-permute-start(bf16[448,384]{1,0:T(8,128)(2,1)S(1)} %bitcast.44), channel_id=1, source_target_pairs={{0,2},{1,3},{2,4},{3,5},{4,6},{5,7},{6,0},{7,1},{8,10},{9,11},{10,... | collective-permute-start | bytes 1032200 | tf_op jit(solution)/shard_map/ppermute | solution.py:247
  83.1 17.0 %collective-permute-start.12 = (bf16[448,384]{1,0:T(8,128)(2,1)S(1)}, bf16[448,384]{1,0:T(8,128)(2,1)}, u32[]{:S(2)}, u32[]{:S(2)}) collective-permute-start(bf16[448,384]{1,0:T(8,128)(2,1)S(1)} %bitcast.45), channel_id=1, source_target_pairs={{0,4},{1,5},{2,6},{3,7},{4,0},{5,1},{6,2},{7,3},{8,12},{9,13},{10,... | collective-permute-start | bytes 1032200 | tf_op jit(solution)/shard_map/ppermute | solution.py:247
  87.2 14.7 %collective-permute-start.13 = (bf16[448,384]{1,0:T(8,128)(2,1)S(1)}, bf16[448,384]{1,0:T(8,128)(2,1)}, u32[]{:S(2)}, u32[]{:S(2)}) collective-permute-start(bf16[448,384]{1,0:T(8,128)(2,1)S(1)} %bitcast.46), channel_id=1, source_target_pairs={{0,6},{1,7},{2,0},{3,1},{4,2},{5,3},{6,4},{7,5},{8,14},{9,15},{10,... | collective-permute-start | bytes 1032200 | tf_op jit(solution)/shard_map/ppermute | solution.py:247
  99.1 6.9 %copy-start.5 = (f32[768]{0:T(1024)S(1)}, f32[768]{0:T(1024)}, u32[]{:S(2)}) copy-start(f32[768]{0:T(1024)} %param.13) | copy-start | bytes 9220
  104.1 12.5 %collective-permute-start.14 = (bf16[1344,384]{1,0:T(8,128)(2,1)}, bf16[1344,384]{1,0:T(8,128)(2,1)}, u32[]{:S(2)}, u32[]{:S(2)}) collective-permute-start(bf16[1344,384]{1,0:T(8,128)(2,1)} %pad_maximum_fusion), channel_id=1, source_target_pairs={{0,1},{1,0},{2,3},{3,2},{4,5},{5,4},{6,7},{7,6},{8,9},{9,8},{10,11... | collective-permute-start | bytes 3096584 | tf_op jit(solution)/shard_map/ppermute | solution.py:256
  106.1 10.5 %all-to-all-start.2 = ((bf16[4,192,128]{2,1,0:T(8,128)(2,1)}), bf16[4,192,128]{2,1,0:T(8,128)(2,1)S(1)}, u32[]{:S(2)}, u32[]{:S(2)}) async-start(bf16[4,192,128]{2,1,0:T(8,128)(2,1)} %conv_block.1), calls=%async_computation.2 | async-start | bytes 393216 | tf_op jit(solution)/shard_map/all_to_all | solution.py:258
  120.4 33.7 %all-to-all-start.3 = ((bf16[16,224,128]{2,1,0:T(8,128)(2,1)}), bf16[16,224,128]{2,1,0:T(8,128)(2,1)S(1)}, u32[]{:S(2)}, u32[]{:S(2)}) async-start(bf16[16,224,128]{2,1,0:T(8,128)(2,1)} %get-tuple-element.27), calls=%async_computation.3 | async-start | bytes 1835008 | tf_op jit(solution)/shard_map/all_to_all | solution.py:260
  (2 other events, 7.9 us)
